TPU v7x, 32 devices: a whole 2x2x4 slice. The times are simulated.
32 devices in a mesh: fsdp: 2 (over core), ctx: 4 (over y, x), tp: 4 (over z).
Axes of the slice: x: 2, y: 2, z: 4, core: 2. Of those that a mesh axis runs over, the one named last changes fastest.
Arguments:
- x_prompt: bfloat16 [2, 1024, 1024], P('fsdp', 'ctx'), may hold values from -6 to 6
- x_cont: bfloat16 [2, 12, 256, 1024], P('fsdp', 'ctx'), may hold values from -6 to 6
- cont_start: int32 [2, 12], P('fsdp', 'ctx'), may hold values from 512 to 1024
- w_qkv: bfloat16 [1024, 3, 1024], P(('fsdp', 'ctx'), None, 'tp'), may hold values from -0.1875 to 0.1875
- qkv_bias: bfloat16 [3, 1024], P(None, 'tp'), may hold values from -3 to 3
- w_dense: bfloat16 [1024, 1024], P('tp', ('fsdp', 'ctx')), may hold values from -0.75 to 0.75
- dense_bias: bfloat16 [1024], P(('fsdp', 'ctx')), may hold values from -3 to 3
- w_fc1: bfloat16 [1024, 4096], P(('fsdp', 'ctx'), 'tp'), may hold values from -0.1875 to 0.1875
- fc1_bias: bfloat16 [4096], P('tp'), may hold values from -3 to 3
- w_fc2: bfloat16 [4096, 1024], P('tp', ('fsdp', 'ctx')), may hold values from -0.09375 to 0.09375
- fc2_bias: bfloat16 [1024], P(('fsdp', 'ctx')), may hold values from -3 to 3
- ln1_gain: bfloat16 [1024], P(('fsdp', 'ctx')), may hold values from 0.099609375 to 1.8984375
- ln1_bias: bfloat16 [1024], P(('fsdp', 'ctx')), may hold values from -2 to 2
- ln2_gain: bfloat16 [1024], P(('fsdp', 'ctx')), may hold values from 0.099609375 to 1.8984375
- ln2_bias: bfloat16 [1024], P(('fsdp', 'ctx')), may hold values from -2 to 2
- dy_prompt: bfloat16 [2, 1024, 1024], P('fsdp', 'ctx'), may hold values from -6 to 6
- dy_cont: bfloat16 [2, 12, 256, 1024], P('fsdp', 'ctx'), may hold values from -6 to 6
Outputs:
- y_prompt: float32 [2, 1024, 1024], P('fsdp', 'ctx')
- y_cont: float32 [2, 12, 256, 1024], P('fsdp', 'ctx')
- dx_prompt: float32 [2, 1024, 1024], P('fsdp', 'ctx')
- dx_cont: float32 [2, 12, 256, 1024], P('fsdp', 'ctx')
- d_w_qkv: float32 [1024, 3, 1024], P(('fsdp', 'ctx'), None, 'tp')
- d_qkv_bias: float32 [3, 1024], P(None, 'tp')
- d_w_dense: float32 [1024, 1024], P('tp', ('fsdp', 'ctx'))
- d_dense_bias: float32 [1024], P(('fsdp', 'ctx'))
- d_w_fc1: float32 [1024, 4096], P(('fsdp', 'ctx'), 'tp')
- d_fc1_bias: float32 [4096], P('tp')
- d_w_fc2: float32 [4096, 1024], P('tp', ('fsdp', 'ctx'))
- d_fc2_bias: float32 [1024], P(('fsdp', 'ctx'))
- d_ln1_gain: float32 [1024], P(('fsdp', 'ctx'))
- d_ln1_bias: float32 [1024], P(('fsdp', 'ctx'))
- d_ln2_gain: float32 [1024], P(('fsdp', 'ctx'))
- d_ln2_bias: float32 [1024], P(('fsdp', 'ctx'))
Inputs may be any that keep to these rules, and one draw needn't show every extreme that they name: `cont_start`: a continuation follows the prompt tokens before its first position.
All inputs are finite; a program needn't handle non-finite values.
Results may differ from a plain program's by a relative error of at most 0.012.
Values may be sent and summed in bfloat16 or wider, within the bound.
A program may use at most 192 MiB of HBM per device.

v0:
```python
import jax
import jax.numpy as jnp
from jax import lax
from jax.sharding import PartitionSpec as P

HD = 64
ROT = 16


EPS = 1e-05


def layer_norm(inputs, norm_gain, norm_shift):
    row_mean = jnp.mean(inputs, axis=-1, keepdims=True)
    centered = inputs - row_mean
    variance = jnp.mean(centered * centered, axis=-1, keepdims=True)
    return centered * lax.rsqrt(variance + EPS) * norm_gain + norm_shift


def norm_pair(inputs, gain_one, shift_one, gain_two, shift_two):
    return (layer_norm(inputs, gain_one, shift_one), layer_norm(inputs, gain_two, shift_two))


def exact_gelu(values):
    return jax.nn.gelu(values, approximate=False)


def rotary_tables(positions):
    freq_index = jnp.arange(ROT // 2).astype(jnp.float32)
    inverse = jnp.power(10000.0, -2.0 * freq_index / ROT)
    phase = positions.astype(jnp.float32)[..., None] * inverse
    cos_half = jnp.cos(phase)
    sin_half = jnp.sin(phase)
    return (
        jnp.concatenate([cos_half, cos_half], axis=-1),
        jnp.concatenate([sin_half, sin_half], axis=-1),
    )


def rotate(inputs, cos_t, sin_t):
    leading = inputs[..., :ROT]
    half_rot = ROT // 2
    turned = jnp.concatenate([-leading[..., half_rot:], leading[..., :half_rot]], axis=-1)
    return jnp.concatenate([leading * cos_t + turned * sin_t, inputs[..., ROT:]], axis=-1)


def masked_scores(
    queries, all_keys, key_limit, query_slot, query_offs, prompt_len, key_slot, key_offs
):
    raw_scores = jnp.einsum("qhd,khd->hqk", queries, all_keys, preferred_element_type=jnp.float32)
    key_index = jnp.arange(all_keys.shape[0], dtype=jnp.int32)
    near_keys = key_index[None, :] < key_limit[:, None]
    own_keys = (key_slot[None, :] == query_slot[:, None]) & (
        key_offs[None, :] <= query_offs[:, None]
    )
    allowed = jnp.where((key_index < prompt_len)[None, :], near_keys, own_keys)
    return jnp.where(allowed[None], raw_scores * 0.125, -1e30)


def on_device(
    x_prompt,
    x_cont,
    cont_start,
    w_qkv,
    qkv_bias,
    w_dense,
    dense_bias,
    w_fc1,
    fc1_bias,
    w_fc2,
    fc2_bias,
    ln1_gain,
    ln1_bias,
    ln2_gain,
    ln2_bias,
    dy_prompt,
    dy_cont,
):
    gathered = (
        lax.all_gather(w_qkv, ("fsdp", "ctx"), axis=0, tiled=True),
        lax.all_gather(w_dense, ("fsdp", "ctx"), axis=1, tiled=True),
        lax.all_gather(w_fc1, ("fsdp", "ctx"), axis=0, tiled=True),
        lax.all_gather(w_fc2, ("fsdp", "ctx"), axis=1, tiled=True),
        lax.all_gather(dense_bias, ("fsdp", "ctx"), axis=0, tiled=True),
        lax.all_gather(fc2_bias, ("fsdp", "ctx"), axis=0, tiled=True),
        lax.all_gather(ln1_gain, ("fsdp", "ctx"), axis=0, tiled=True),
        lax.all_gather(ln1_bias, ("fsdp", "ctx"), axis=0, tiled=True),
        lax.all_gather(ln2_gain, ("fsdp", "ctx"), axis=0, tiled=True),
        lax.all_gather(ln2_bias, ("fsdp", "ctx"), axis=0, tiled=True),
    )
    qkv_full, dense_full, up_full, down_full = (gathered[0], gathered[1], gathered[2], gathered[3])
    dense_shift = gathered[4].astype(jnp.float32)
    down_shift = gathered[5].astype(jnp.float32)
    gain_one = gathered[6].astype(jnp.float32)
    shift_one = gathered[7].astype(jnp.float32)
    gain_two = gathered[8].astype(jnp.float32)
    shift_two = gathered[9].astype(jnp.float32)
    p_rows = x_prompt.shape[1]
    cont_count = x_cont.shape[1]
    cont_len = x_cont.shape[2]
    model_width = x_prompt.shape[2]
    row_count = p_rows + cont_count * cont_len
    prompt_len = p_rows * lax.axis_size("ctx")
    local_cols = qkv_full.shape[2]
    head_count = local_cols // HD
    piece_index = lax.axis_index("ctx")
    inputs = jnp.concatenate(
        [x_prompt[0], x_cont[0].reshape(cont_count * cont_len, model_width)], axis=0
    ).astype(jnp.float32)
    offsets = jnp.arange(cont_len, dtype=jnp.int32)
    prompt_pos = piece_index * p_rows + jnp.arange(p_rows, dtype=jnp.int32)
    starts = cont_start[0]
    cont_pos = (starts[:, None] + offsets[None, :]).reshape(cont_count * cont_len)
    positions = jnp.concatenate([prompt_pos, cont_pos])
    key_limit = jnp.concatenate([prompt_pos + 1, jnp.repeat(starts, cont_len)])
    own_slot = jnp.repeat(jnp.arange(cont_count, dtype=jnp.int32), cont_len)
    own_offs = jnp.tile(offsets, cont_count)
    query_slot = jnp.concatenate([jnp.full((p_rows,), -1, jnp.int32), own_slot])
    query_offs = jnp.concatenate([jnp.zeros((p_rows,), jnp.int32), own_offs])
    key_slot = jnp.concatenate([jnp.full((prompt_len,), -1, jnp.int32), own_slot])
    key_offs = jnp.concatenate([jnp.zeros((prompt_len,), jnp.int32), own_offs])
    cos_t, sin_t = rotary_tables(positions)
    cos_t = cos_t[:, None, :]
    sin_t = sin_t[:, None, :]
    norm_one, norm_two = norm_pair(inputs, gain_one, shift_one, gain_two, shift_two)
    ln_one = norm_one.astype(jnp.bfloat16)
    ln_two = norm_two.astype(jnp.bfloat16)
    qkv_flat = qkv_full.reshape(model_width, 3 * local_cols)
    projected = jnp.dot(ln_one, qkv_flat, preferred_element_type=jnp.float32) + qkv_bias.reshape(
        3 * local_cols
    ).astype(jnp.float32)
    projected = projected.reshape(row_count, 3, head_count, HD)
    queries = rotate(projected[:, 0], cos_t, sin_t).astype(jnp.bfloat16)
    keys_own = rotate(projected[:, 1], cos_t, sin_t).astype(jnp.bfloat16)
    values_own = projected[:, 2].astype(jnp.bfloat16)
    prompt_keys, prompt_values = (
        lax.all_gather(keys_own[:p_rows].reshape(p_rows, local_cols), "ctx", axis=0, tiled=True),
        lax.all_gather(values_own[:p_rows].reshape(p_rows, local_cols), "ctx", axis=0, tiled=True),
    )
    all_keys = jnp.concatenate(
        [prompt_keys.reshape(prompt_len, head_count, HD), keys_own[p_rows:]], axis=0
    )
    all_values = jnp.concatenate(
        [prompt_values.reshape(prompt_len, head_count, HD), values_own[p_rows:]], axis=0
    )
    scores = masked_scores(
        queries, all_keys, key_limit, query_slot, query_offs, prompt_len, key_slot, key_offs
    )
    highest = jnp.max(scores, axis=-1, keepdims=True)
    log_total = highest + jnp.log(jnp.sum(jnp.exp(scores - highest), axis=-1, keepdims=True))
    probs_low = jnp.exp(scores - log_total).astype(jnp.bfloat16)
    attended = jnp.einsum("hqk,khd->qhd", probs_low, all_values, preferred_element_type=jnp.float32)
    attended_low = attended.reshape(row_count, local_cols).astype(jnp.bfloat16)
    attn_part = jnp.dot(attended_low, dense_full, preferred_element_type=jnp.float32)
    hidden = jnp.dot(ln_two, up_full, preferred_element_type=jnp.float32) + fc1_bias.astype(
        jnp.float32
    )
    active_low = exact_gelu(hidden).astype(jnp.bfloat16)
    mlp_part = jnp.dot(active_low, down_full, preferred_element_type=jnp.float32)
    attn_total = lax.psum(attn_part, "tp")
    mlp_total = lax.psum(mlp_part.astype(jnp.bfloat16), "tp").astype(jnp.float32)
    mixed = attn_total + mlp_total
    output = inputs + mixed + dense_shift + down_shift
    again = (
        lax.all_gather(w_qkv, ("fsdp", "ctx"), axis=0, tiled=True),
        lax.all_gather(w_dense, ("fsdp", "ctx"), axis=1, tiled=True),
        lax.all_gather(w_fc1, ("fsdp", "ctx"), axis=0, tiled=True),
        lax.all_gather(w_fc2, ("fsdp", "ctx"), axis=1, tiled=True),
    )
    qkv_flat = again[0].reshape(model_width, 3 * local_cols)
    dense_full, up_full, down_full = (again[1], again[2], again[3])
    grad_out = jnp.concatenate(
        [dy_prompt[0], dy_cont[0].reshape(cont_count * cont_len, model_width)], axis=0
    )
    grad_dense = jnp.dot(attended_low.T, grad_out, preferred_element_type=jnp.float32)
    grad_down = jnp.dot(active_low.T, grad_out, preferred_element_type=jnp.float32)
    grad_shift = jnp.sum(grad_out.astype(jnp.float32), axis=0)
    grad_attended = (
        jnp.dot(grad_out, dense_full.T, preferred_element_type=jnp.float32)
        .astype(jnp.bfloat16)
        .reshape(row_count, head_count, HD)
    )
    scores = masked_scores(
        queries, all_keys, key_limit, query_slot, query_offs, prompt_len, key_slot, key_offs
    )
    probs = jnp.exp(scores - log_total)
    probs_low = probs.astype(jnp.bfloat16)
    grad_probs = jnp.einsum(
        "qhd,khd->hqk", grad_attended, all_values, preferred_element_type=jnp.float32
    )
    inner = jnp.sum(probs * grad_probs, axis=-1, keepdims=True)
    grad_scores = (probs * (grad_probs - inner)).astype(jnp.bfloat16)
    grad_queries = (
        jnp.einsum("hqk,khd->qhd", grad_scores, all_keys, preferred_element_type=jnp.float32)
        * 0.125
    )
    grad_keys = (
        jnp.einsum("hqk,qhd->khd", grad_scores, queries, preferred_element_type=jnp.float32) * 0.125
    )
    grad_values = jnp.einsum(
        "hqk,qhd->khd", probs_low, grad_attended, preferred_element_type=jnp.float32
    )
    prompt_key_grads, prompt_value_grads = (
        lax.psum_scatter(
            grad_keys[:prompt_len].reshape(prompt_len, local_cols),
            "ctx",
            scatter_dimension=0,
            tiled=True,
        ),
        lax.psum_scatter(
            grad_values[:prompt_len].reshape(prompt_len, local_cols),
            "ctx",
            scatter_dimension=0,
            tiled=True,
        ),
    )
    grad_keys = jnp.concatenate(
        [prompt_key_grads.reshape(p_rows, head_count, HD), grad_keys[prompt_len:]], axis=0
    )
    grad_values = jnp.concatenate(
        [prompt_value_grads.reshape(p_rows, head_count, HD), grad_values[prompt_len:]], axis=0
    )
    grad_projected = jnp.stack(
        [rotate(grad_queries, cos_t, -sin_t), rotate(grad_keys, cos_t, -sin_t), grad_values], axis=1
    )
    grad_proj_low = grad_projected.reshape(row_count, 3 * local_cols).astype(jnp.bfloat16)
    grad_qkv = jnp.dot(ln_one.T, grad_proj_low, preferred_element_type=jnp.float32).reshape(
        model_width, 3, local_cols
    )
    grad_qkv_bias = jnp.sum(grad_proj_low.astype(jnp.float32), axis=0).reshape(3, local_cols)
    grad_norm_one = jnp.dot(grad_proj_low, qkv_flat.T, preferred_element_type=jnp.float32)
    grad_active = jnp.dot(grad_out, down_full.T, preferred_element_type=jnp.float32)
    gelu_back = jax.vjp(exact_gelu, hidden)[1]
    grad_hidden_low = gelu_back(grad_active)[0].astype(jnp.bfloat16)
    grad_up = jnp.dot(ln_two.T, grad_hidden_low, preferred_element_type=jnp.float32)
    grad_up_bias = jnp.sum(grad_hidden_low.astype(jnp.float32), axis=0)
    grad_norm_two = jnp.dot(grad_hidden_low, up_full.T, preferred_element_type=jnp.float32)
    norm_back = jax.vjp(norm_pair, inputs, gain_one, shift_one, gain_two, shift_two)[1]
    full_one = lax.psum(grad_norm_one, "tp")
    full_two = lax.psum(grad_norm_two, "tp")
    grad_in, grad_gain_one, grad_shift_one, grad_gain_two, grad_shift_two = norm_back(
        (full_one, full_two)
    )
    grad_inputs = grad_in + grad_out.astype(jnp.float32)
    owned = (
        lax.psum_scatter(grad_qkv, ("fsdp", "ctx"), scatter_dimension=0, tiled=True),
        lax.psum_scatter(grad_dense, ("fsdp", "ctx"), scatter_dimension=1, tiled=True),
        lax.psum_scatter(grad_up, ("fsdp", "ctx"), scatter_dimension=0, tiled=True),
        lax.psum_scatter(grad_down, ("fsdp", "ctx"), scatter_dimension=1, tiled=True),
        lax.psum_scatter(grad_shift, ("fsdp", "ctx"), scatter_dimension=0, tiled=True),
        lax.psum_scatter(grad_gain_one, ("fsdp", "ctx"), scatter_dimension=0, tiled=True),
        lax.psum_scatter(grad_shift_one, ("fsdp", "ctx"), scatter_dimension=0, tiled=True),
        lax.psum_scatter(grad_gain_two, ("fsdp", "ctx"), scatter_dimension=0, tiled=True),
        lax.psum_scatter(grad_shift_two, ("fsdp", "ctx"), scatter_dimension=0, tiled=True),
    )
    bias_qkv_total, bias_up_total = lax.psum((grad_qkv_bias, grad_up_bias), ("fsdp", "ctx"))
    y_prompt = output[:p_rows][None]
    y_cont = output[p_rows:].reshape(1, cont_count, cont_len, model_width)
    dx_prompt = grad_inputs[:p_rows][None]
    dx_cont = grad_inputs[p_rows:].reshape(1, cont_count, cont_len, model_width)
    return (
        y_prompt,
        y_cont,
        dx_prompt,
        dx_cont,
        owned[0],
        bias_qkv_total,
        owned[1],
        owned[4],
        owned[2],
        bias_up_total,
        owned[3],
        owned[4],
        owned[5],
        owned[6],
        owned[7],
        owned[8],
    )


def solution(mesh):
    placed = (
        P("fsdp", "ctx", None),
        P("fsdp", "ctx", None, None),
        P("fsdp", "ctx"),
        P(("fsdp", "ctx"), None, "tp"),
        P(None, "tp"),
        P("tp", ("fsdp", "ctx")),
        P(("fsdp", "ctx")),
        P(("fsdp", "ctx"), "tp"),
        P("tp"),
        P("tp", ("fsdp", "ctx")),
        P(("fsdp", "ctx")),
        P(("fsdp", "ctx")),
        P(("fsdp", "ctx")),
        P(("fsdp", "ctx")),
        P(("fsdp", "ctx")),
        P("fsdp", "ctx", None),
        P("fsdp", "ctx", None, None),
    )
    return jax.shard_map(
        on_device,
        mesh=mesh,
        in_specs=placed,
        out_specs=(
            P("fsdp", "ctx", None),
            P("fsdp", "ctx", None, None),
            P("fsdp", "ctx", None),
            P("fsdp", "ctx", None, None),
            P(("fsdp", "ctx"), None, "tp"),
            P(None, "tp"),
            P("tp", ("fsdp", "ctx")),
            P(("fsdp", "ctx")),
            P(("fsdp", "ctx"), "tp"),
            P("tp"),
            P("tp", ("fsdp", "ctx")),
            P(("fsdp", "ctx")),
            P(("fsdp", "ctx")),
            P(("fsdp", "ctx")),
            P(("fsdp", "ctx")),
            P(("fsdp", "ctx")),
        ),
        check_vma=False,
    )
```

profile of v0, /device:TPU:0, one launch (start us, length us, event | category | flops | bytes accessed | tf_op | source)
XLA Modules:
  0.0 1037.2 jit_solution(66057958732764653)
XLA Ops:
  18.0 14.7 %all-gather = bf16[8,1,128]{2,1,0:T(2,128)(2,1)S(1)} all-gather(bf16[1,1,128]{2,1,0:T(2,128)(2,1)S(1)} %bitcast.150), channel_id=1, replica_groups=mesh['fsdp'=2,'ctx'=4,'tp'=4] {'fsdp','ctx'}, dimensions={0}, use_global_device_ids=true | all-gather | bytes 2304 | tf_op jit(solution)/shard_map/all_gather | solution.py:86
  32.7 13.2 %all-gather.1 = bf16[8,1,128]{2,1,0:T(2,128)(2,1)S(1)} all-gather(bf16[1,1,128]{2,1,0:T(2,128)(2,1)S(1)} %bitcast.151), channel_id=1, replica_groups=mesh['fsdp'=2,'ctx'=4,'tp'=4] {'fsdp','ctx'}, dimensions={0}, use_global_device_ids=true | all-gather | bytes 2304 | tf_op jit(solution)/shard_map/all_gather | solution.py:87
  48.1 25.5 %all_gather.45 = bf16[256,1024]{1,0:T(8,128)(2,1)S(1)} all-gather(bf16[256,128]{1,0:T(8,128)(2,1)S(1)} %copy-done.22), channel_id=1, replica_groups=mesh['fsdp'=2,'ctx'=4,'tp'=4] {'fsdp','ctx'}, dimensions={1}, use_global_device_ids=true | all-gather | bytes 589824 | tf_op jit(solution)/shard_map/all_gather | solution.py:81
  73.6 12.2 %all-gather.2 = bf16[8,1,128]{2,1,0:T(2,128)(2,1)S(1)} all-gather(bf16[1,1,128]{2,1,0:T(2,128)(2,1)S(1)} %bitcast.153), channel_id=1, replica_groups=mesh['fsdp'=2,'ctx'=4,'tp'=4] {'fsdp','ctx'}, dimensions={0}, use_global_device_ids=true | all-gather | bytes 2304 | tf_op jit(solution)/shard_map/all_gather | solution.py:88
  85.8 13.8 %all-gather.3 = bf16[8,1,128]{2,1,0:T(2,128)(2,1)S(1)} all-gather(bf16[1,1,128]{2,1,0:T(2,128)(2,1)S(1)} %bitcast.154), channel_id=1, replica_groups=mesh['fsdp'=2,'ctx'=4,'tp'=4] {'fsdp','ctx'}, dimensions={0}, use_global_device_ids=true | all-gather | bytes 2304 | tf_op jit(solution)/shard_map/all_gather | solution.py:89
  111.9 12.9 %all_gather.44 = bf16[1024,256]{0,1:T(8,128)(2,1)S(1)} all-gather(bf16[256,256]{0,1:T(8,128)(2,1)S(1)} %bitcast.131), channel_id=1, replica_groups=mesh['fsdp'=2,'ctx'=4,'tp'=4] {'ctx'}, dimensions={0}, use_global_device_ids=true | all-gather | bytes 655360 | tf_op jit(solution)/shard_map/all_gather | solution.py:137
  124.8 12.9 %fusion = (f32[4,1024]{1,0:T(4,128)S(1)}, f32[4,1024,1792]{2,1,0:T(8,128)}) fusion(pred[1024,1792]{1,0:T(8,128)(4,1)S(1)} %fusion.2, bf16[1024,4,48]{0,2,1:T(8,128)(2,1)S(1)} %slice.216, bf16[1024,4,16]{0,2,1:T(8,128)(2,1)S(1)} %get-tuple-element.57, bf16[1024,4,64]{0,2,1:T(8,128)(2,1)S(1)} %bitcast.123, bf16[1024,4,48]{0,2,1:T(8,128)(2,1)S(1)} %slice.217, ...), kind=kOutput, calls=%fused_computation.5 | convolution fusion | flops 966717440 | bytes 32784384 | tf_op jit(solution)/shard_map/qhd,khd->hqk/dot_general | solution.py:50
  137.6 13.8 %exponential_reduce_fusion = f32[4,1024]{1,0:T(4,128)S(1)} fusion(f32[4,1024,1792]{2,1,0:T(8,128)} %get-tuple-element.66, f32[4,1024]{1,0:T(4,128)S(1)} %get-tuple-element.65, pred[1024,1792]{1,0:T(8,128)(4,1)S(1)} %fusion.2), kind=kLoop, calls=%fused_computation.3 | loop fusion | flops 29356032 | bytes 31227904 | tf_op jit(solution)/shard_map/reduce_sum | solution.py:150
  151.4 12.7 %all_gather.43 = bf16[1024,256]{0,1:T(8,128)(2,1)S(1)} all-gather(bf16[256,256]{0,1:T(8,128)(2,1)S(1)} %bitcast.132), channel_id=1, replica_groups=mesh['fsdp'=2,'ctx'=4,'tp'=4] {'ctx'}, dimensions={0}, use_global_device_ids=true | all-gather | bytes 655360 | tf_op jit(solution)/shard_map/all_gather | solution.py:138
  164.2 22.0 %multiply_reduce_fusion = (f32[4,1024]{1,0:T(4,128)S(1)}, f32[4,1024,1792]{2,1,0:T(8,128)}) fusion(f32[4,1024,1792]{2,1,0:T(8,128)} %get-tuple-element.66, f32[4,1024]{1,0:T(4,128)S(1)} %log_add_fusion, pred[1024,1792]{1,0:T(8,128)(4,1)S(1)} %fusion.2, bf16[1024,4,64]{0,2,1:T(8,128)(2,1)S(1)} %bitcast.129, bf16[768,4,64]{0,2,1:T(8,128)(2,1)S(1)} %slice_bitcast_fusion.4, ...), kind=kOutput, calls=%fused_computation.1 | convolution fusion | flops 978055168 | bytes 62029824 | tf_op jit(solution)/shard_map/qhd,khd->hqk/dot_general | solution.py:188
  186.2 24.6 %multiply_convert_fusion = bf16[4,1024,1792]{2,1,0:T(8,128)(2,1)} fusion(f32[4,1024,1792]{2,1,0:T(8,128)} %get-tuple-element.69, f32[4,1024,1792]{2,1,0:T(8,128)} %get-tuple-element.66, f32[4,1024]{1,0:T(4,128)S(1)} %get-tuple-element.68, f32[4,1024]{1,0:T(4,128)S(1)} %log_add_fusion, pred[1024,1792]{1,0:T(8,128)(4,1)S(1)} %fusion.2), kind=kLoop, calls=%fused_computation | loop fusion | flops 44040192 | bytes 75268096 | tf_op jit(solution)/shard_map/convert_element_type | solution.py:192
  220.7 12.7 %convolution_bitcast_fusion = f32[1792,4,64]{0,2,1:T(8,128)S(1)} fusion(bf16[1024,4,64]{0,2,1:T(8,128)(2,1)S(1)} %bitcast.130, f32[4,1024,1792]{2,1,0:T(8,128)} %get-tuple-element.66, f32[4,1024]{1,0:T(4,128)S(1)} %log_add_fusion, pred[1024,1792]{1,0:T(8,128)(4,1)S(1)} %fusion.2), kind=kOutput, calls=%fused_computation.58 | convolution fusion | flops 968884224 | bytes 33570816 | tf_op jit(solution)/shard_map/hqk,qhd->khd/dot_general | solution.py:200
  235.3 9.7 fusion.35
  246.9 14.3 %convolution_convert_fusion.1 = bf16[4,64,1024]{2,1,0:T(8,128)(2,1)} fusion(bf16[768,4,64]{0,2,1:T(8,128)(2,1)} %copy-done.13, bf16[1024,4,64]{0,2,1:T(8,128)(2,1)} %bitcast.117, f32[4,1024,1792]{2,1,0:T(8,128)} %get-tuple-element.66, f32[4,1024]{1,0:T(4,128)S(1)} %log_add_fusion, pred[1024,1792]{1,0:T(8,128)(4,1)S(1)} %fusion.2), kind=kOutput, calls=%fused_computation.75 | convolution fusion | flops 970981376 | bytes 32653312 | tf_op jit(solution)/shard_map/hqk,khd->qhd/dot_general | solution.py:152
  265.5 16.0 %multiply_convert_fusion.1 = (bf16[1024,1024]{1,0:T(8,128)(2,1)}, f32[1024,1024]{1,0:T(8,128)}, f32[1024,1024]{1,0:T(8,128)}) fusion(f32[1024]{0:T(1024)S(1)} %copy-done.26, bf16[1024,1024]{1,0:T(8,128)(2,1)} %all-gather.12.cloned.1.call-done, f32[1024]{0:T(1024)S(1)} %bitcast.148, f32[1024]{0:T(1024)S(1)} %bitcast.139, f32[1024]{0:T(1024)S(1)} %fusion.55, ...), kind=kOutput, calls=%fused_computation.41 | convolution fusion | flops 2226126848 | bytes 14700544 | tf_op jit(solution)/shard_map/dot_general | solution.py:155
  341.5 13.7 %all-gather.4 = bf16[8,1,128]{2,1,0:T(2,128)(2,1)S(1)} all-gather(bf16[1,1,128]{2,1,0:T(2,128)(2,1)S(1)} %bitcast.155), channel_id=1, replica_groups=mesh['fsdp'=2,'ctx'=4,'tp'=4] {'fsdp','ctx'}, dimensions={0}, use_global_device_ids=true | all-gather | bytes 2304 | tf_op jit(solution)/shard_map/all_gather | solution.py:84
  355.2 13.4 %all-gather.5 = bf16[8,1,128]{2,1,0:T(2,128)(2,1)S(1)} all-gather(bf16[1,1,128]{2,1,0:T(2,128)(2,1)S(1)} %bitcast.156), channel_id=1, replica_groups=mesh['fsdp'=2,'ctx'=4,'tp'=4] {'fsdp','ctx'}, dimensions={0}, use_global_device_ids=true | all-gather | bytes 2304 | tf_op jit(solution)/shard_map/all_gather | solution.py:85
  369.8 370.8 %all-reduce.16.cloned.1.call-done = (f32[1024,1024]{1,0:T(8,128)}, f32[1024,1024]{1,0:T(8,128)}, f32[1024,1024]{1,0:T(8,128)}) async-done(((f32[1024,1024]{1,0:T(8,128)}, f32[1024,1024]{1,0:T(8,128)}, f32[1024,1024]{1,0:T(8,128)}), (f32[1024,1024]{1,0:T(8,128)}, f32[1024,1024]{1,0:T(8,128)}, f32[1024,1024]{1,0:T(8,128)})) %all-reduce.16.cloned.1.call-update) | async-done | bytes 12582928 | tf_op jit(solution)/shard_map/psum | solution.py:160
  745.4 83.7 %all-reduce.14.cloned.1.call-done = bf16[1024,1024]{1,0:T(8,128)(2,1)} async-done(((bf16[1024,1024]{1,0:T(8,128)(2,1)}), bf16[1024,1024]{1,0:T(8,128)(2,1)}) %all-reduce.14.cloned.1.call-update) | async-done | bytes 2097168 | tf_op jit(solution)/shard_map/psum | solution.py:161
  829.1 9.3 fusion.18
  843.8 26.6 %all-reduce.9 = (f32[3,256]{1,0:T(4,128)}, f32[1024]{0:T(1024)S(1)}, f32[1024]{0:T(1024)}, f32[1024]{0:T(1024)S(1)}, f32[1024]{0:T(1024)S(1)}, /*index=5*/f32[1024]{0:T(1024)S(1)}, f32[1024]{0:T(1024)S(1)}) all-reduce(f32[3,256]{1,0:T(4,128)S(1)} %reshape.336, ...), channel_id=1, replica_groups=mesh['fsdp'=2,'ctx'=4,'tp'=4] {'fsdp','ctx'}, use_global_device_ids=true, to_apply=%region_17.18 | all-reduce | flops 6912 | bytes 55296 | tf_op jit(solution)/shard_map/psum | solution.py:256
  882.0 36.9 %reduce-scatter.11.cloned.1.call-done = f32[128,3,256]{2,0,1:T(8,128)} async-done(((f32[1024,3,256]{2,0,1:T(8,128)}), f32[128,3,256]{2,0,1:T(8,128)}) %reduce-scatter.11.cloned.1.call-update) | async-done | bytes 393232 | tf_op jit(solution)/shard_map/reduce_scatter | solution.py:246
  919.0 55.1 %reduce-scatter.15.cloned.1.call-done = f32[128,1024]{1,0:T(8,128)} async-done(((f32[1024,1024]{1,0:T(8,128)}), f32[128,1024]{1,0:T(8,128)}) %reduce-scatter.15.cloned.1.call-update) | async-done | bytes 524304 | tf_op jit(solution)/shard_map/reduce_scatter | solution.py:248
  974.1 55.6 %reduce-scatter.17.cloned.1.call-done = f32[1024,128]{1,0:T(8,128)} async-done(((f32[1024,1024]{1,0:T(8,128)}), f32[1024,128]{1,0:T(8,128)}) %reduce-scatter.17.cloned.1.call-update) | async-done | bytes 524304 | tf_op jit(solution)/shard_map/reduce_scatter | solution.py:249
  (200 shorter events, 125.5 us)
Async XLA Ops:
  7.2 39.3 %copy-start.30 = (bf16[3,256]{1,0:T(4,128)(2,1)S(1)}, bf16[3,256]{1,0:T(4,128)(2,1)}, u32[]{:S(2)}) copy-start(bf16[3,256]{1,0:T(4,128)(2,1)} %param.21) | copy-start | bytes 4612
  7.2 39.9 %copy-start.34 = (s32[1,3]{1,0:T(1,128)S(1)}, s32[1,3]{1,0:T(1,128)}, u32[]{:S(2)}) copy-start(s32[1,3]{1,0:T(1,128)} %param.19) | copy-start | bytes 40
  7.2 40.9 %copy-start.22 = (bf16[256,128]{1,0:T(8,128)(2,1)S(1)}, bf16[256,128]{1,0:T(8,128)(2,1)}, u32[]{:S(2)}) copy-start(bf16[256,128]{1,0:T(8,128)(2,1)} %param.22) | copy-start | bytes 196612
  7.2 66.3 %copy-start.35 = (bf16[128]{0:T(256)(128)(2,1)S(1)}, bf16[128]{0:T(256)(128)(2,1)}, u32[]{:S(2)}) copy-start(bf16[128]{0:T(256)(128)(2,1)} %param.30) | copy-start | bytes 772
  7.3 78.6 %copy-start.36 = (bf16[128]{0:T(256)(128)(2,1)S(1)}, bf16[128]{0:T(256)(128)(2,1)}, u32[]{:S(2)}) copy-start(bf16[128]{0:T(256)(128)(2,1)} %param.31) | copy-start | bytes 772
  7.3 93.0 %copy-start.31 = (bf16[1024]{0:T(1024)(128)(2,1)S(1)}, bf16[1024]{0:T(1024)(128)(2,1)}, u32[]{:S(2)}) copy-start(bf16[1024]{0:T(1024)(128)(2,1)} %param.25) | copy-start | bytes 6148
  7.3 93.6 %copy-start.6 = (bf16[1,3,256,1024]{3,2,1,0:T(8,128)(2,1)S(1)}, bf16[1,3,256,1024]{3,2,1,0:T(8,128)(2,1)}, u32[]{:S(2)}) copy-start(bf16[1,3,256,1024]{3,2,1,0:T(8,128)(2,1)} %param.33) | copy-start | bytes 4718596
  7.3 100.1 %all-gather.10.cloned.1.call-start = ((), (), s32[]{:S(2)}) async-start(), calls=%async_computation.6 | async-start | bytes 1769472 | tf_op jit(solution)/shard_map/all_gather | solution.py:80
  9.2 256.2 %all-gather.12.cloned.1.call-start = ((), (), s32[]{:S(2)}) async-start(), calls=%async_computation.7 | async-start | bytes 2359296 | tf_op jit(solution)/shard_map/all_gather | solution.py:82
  10.0 271.5 %all-gather.14.cloned.1.call-start = ((), (), s32[]{:S(2)}) async-start(), calls=%async_computation.8 | async-start | bytes 2359296 | tf_op jit(solution)/shard_map/all_gather | solution.py:83
  10.7 285.6 %reduce-scatter.7.cloned.1.call-start = ((), (), s32[]{:S(2)}) async-start(), calls=%async_computation.10 | async-start | bytes 1310720 | tf_op jit(solution)/shard_map/reduce_scatter | solution.py:204
  32.7 74.7 %copy-start.20 = (f32[8,1,128]{2,1,0:T(1,128)}, f32[8,1,128]{2,1,0:T(1,128)S(1)}, u32[]{:S(2)}) copy-start(f32[8,1,128]{2,1,0:T(1,128)S(1)} %convert_element_type.144) | copy-start | bytes 12292
  48.1 63.7 %copy-start.16 = (f32[1024,16]{0,1:T(8,128)}, f32[1024,16]{0,1:T(8,128)S(1)}, u32[]{:S(2)}) copy-start(f32[1024,16]{0,1:T(8,128)S(1)} %pad_maximum_fusion.9) | copy-start | bytes 196612
  73.6 29.9 %copy-start.11 = (bf16[256,1024]{1,0:T(8,128)(2,1)}, bf16[256,1024]{1,0:T(8,128)(2,1)S(1)}, u32[]{:S(2)}) copy-start(bf16[256,1024]{1,0:T(8,128)(2,1)S(1)} %all_gather.45) | copy-start | bytes 1572868
  111.7 52.4 %copy-start.13 = (bf16[768,4,64]{0,2,1:T(8,128)(2,1)}, bf16[768,4,64]{0,2,1:T(8,128)(2,1)S(1)}, u32[]{:S(2)}) copy-start(bf16[768,4,64]{0,2,1:T(8,128)(2,1)S(1)} %slice_bitcast_fusion.4) | copy-start | bytes 1179652
  246.8 58.7 %reduce-scatter.9.cloned.1.call-start = ((), (), s32[]{:S(2)}) async-start(), calls=%async_computation.11 | async-start | bytes 1310720 | tf_op jit(solution)/shard_map/reduce_scatter | solution.py:210
  265.2 475.5 %all-reduce.16.cloned.1.call-start = ((), (), s32[]{:S(2)}) async-start(), calls=%async_computation.16 | async-start | bytes 25165824 | tf_op jit(solution)/shard_map/psum | solution.py:160
  313.1 516.0 %all-reduce.14.cloned.1.call-start = ((), (), s32[]{:S(2)}) async-start(), calls=%async_computation.9 | async-start | bytes 4194304 | tf_op jit(solution)/shard_map/psum | solution.py:161
  319.4 562.6 %reduce-scatter.13.cloned.1.call-start = ((), (), s32[]{:S(2)}) async-start(), calls=%async_computation.13 | async-start | bytes 1179648 | tf_op jit(solution)/shard_map/reduce_scatter | solution.py:247
  322.7 596.2 %reduce-scatter.11.cloned.1.call-start = ((), (), s32[]{:S(2)}) async-start(), calls=%async_computation.12 | async-start | bytes 3538944 | tf_op jit(solution)/shard_map/reduce_scatter | solution.py:246
  328.1 646.0 %reduce-scatter.15.cloned.1.call-start = ((), (), s32[]{:S(2)}) async-start(), calls=%async_computation.14 | async-start | bytes 4718592 | tf_op jit(solution)/shard_map/reduce_scatter | solution.py:248
  334.4 695.3 %reduce-scatter.17.cloned.1.call-start = ((), (), s32[]{:S(2)}) async-start(), calls=%async_computation.15 | async-start | bytes 4718592 | tf_op jit(solution)/shard_map/reduce_scatter | solution.py:249
  340.8 27.7 %copy-start.41 = (u32[32]{0:T(128)S(1)}, u32[32]{0:T(128)}, u32[]{:S(2)}) copy-start(u32[32]{0:T(128)} %constant.122) | copy-start | bytes 388
  870.5 159.3 %copy-start.42 = (f32[128]{0:T(128)}, f32[128]{0:T(128)S(1)}, u32[]{:S(2)}) copy-start(f32[128]{0:T(128)S(1)} %dynamic-slice.1) | copy-start | bytes 1540
  (31 other events, 237.0 us)
Sparse Core Ops, SparseCore 0:
  10.6 28.5 all-gather.9
  41.1 33.7 all-gather.11
  76.8 28.1 all-gather.13
  246.9 27.1 reduce-scatter.6
  277.7 27.7 reduce-scatter.8
  313.2 427.4 all-reduce.15
  743.6 85.4 all-reduce.13
  833.1 35.1 reduce-scatter.12
  872.7 46.2 reduce-scatter.10
  922.7 51.3 reduce-scatter.14
  978.4 51.2 reduce-scatter.16
where the time goes:
time: 1050 us; the launch traced here: 1040 us
  waiting for transfers between devices  609 us (58%)
  blocking collectives  159 us (15%)
  matrix products  150 us (14%)
  other arithmetic  76 us (7%)
  local copies, waits for them, and re-layouts  27.1 us (3%)
  between operations  15.5 us (1%)
    psum x1, waiting for transfers between devices, on_device(): attn_total = lax.psum(attn_part, 'tp')  371 us
    psum x1, waiting for transfers between devices, on_device(): lax.psum(mlp_part.astype(jnp.bfloat16), 'tp').astype(jnp.float32)  83.7 us
    reduce_scatter x1, waiting for transfers between devices, on_device(): lax.psum_scatter(grad_down, ('fsdp', 'ctx'), scatter_dimension=1, tiled=T...  55.6 us
    reduce_scatter x1, waiting for transfers between devices, on_device(): lax.psum_scatter(grad_up, ('fsdp', 'ctx'), scatter_dimension=0, tiled=True)  55.1 us
    reduce_scatter x1, waiting for transfers between devices, on_device(): lax.psum_scatter(grad_qkv, ('fsdp', 'ctx'), scatter_dimension=0, tiled=True)  36.9 us
    psum x1, blocking collectives, on_device(): lax.psum((grad_qkv_bias, grad_up_bias), ('fsdp', 'ctx'))  26.6 us
    all_gather x1, blocking collectives, on_device(): lax.all_gather(w_dense, ('fsdp', 'ctx'), axis=1, tiled=True)  25.5 us
    convert_element_type x1, other arithmetic, on_device(): grad_scores = (probs * (grad_probs - inner)).astype(jnp.bfloat16)  24.6 us
  transfers between devices with their start and end apart: 11, of which 6 were waited for; matrix products, arithmetic and copies ran while one was open for 23% of the time, Pallas kernels for 0%

commit v1 on v0

--- a/solution.py
+++ b/solution.py
@@ -8,17 +8,6 @@
 
 
 EPS = 1e-05
-
-
-def layer_norm(inputs, norm_gain, norm_shift):
-    row_mean = jnp.mean(inputs, axis=-1, keepdims=True)
-    centered = inputs - row_mean
-    variance = jnp.mean(centered * centered, axis=-1, keepdims=True)
-    return centered * lax.rsqrt(variance + EPS) * norm_gain + norm_shift
-
-
-def norm_pair(inputs, gain_one, shift_one, gain_two, shift_two):
-    return (layer_norm(inputs, gain_one, shift_one), layer_norm(inputs, gain_two, shift_two))
 
 
 def exact_gelu(values):
@@ -122,7 +111,13 @@
     cos_t, sin_t = rotary_tables(positions)
     cos_t = cos_t[:, None, :]
     sin_t = sin_t[:, None, :]
-    norm_one, norm_two = norm_pair(inputs, gain_one, shift_one, gain_two, shift_two)
+    row_mean = jnp.mean(inputs, axis=-1, keepdims=True)
+    centered = inputs - row_mean
+    scale = lax.rsqrt(jnp.mean(centered * centered, axis=-1, keepdims=True) + EPS)
+    unit = centered * scale
+    norm_one = unit * gain_one + shift_one
+    norm_two = unit * gain_two + shift_two
+    unit_low = unit.astype(jnp.bfloat16)
     ln_one = norm_one.astype(jnp.bfloat16)
     ln_two = norm_two.astype(jnp.bfloat16)
     qkv_flat = qkv_full.reshape(model_width, 3 * local_cols)
@@ -157,18 +152,8 @@
     )
     active_low = exact_gelu(hidden).astype(jnp.bfloat16)
     mlp_part = jnp.dot(active_low, down_full, preferred_element_type=jnp.float32)
-    attn_total = lax.psum(attn_part, "tp")
-    mlp_total = lax.psum(mlp_part.astype(jnp.bfloat16), "tp").astype(jnp.float32)
-    mixed = attn_total + mlp_total
+    mixed = lax.psum((attn_part + mlp_part).astype(jnp.bfloat16), "tp").astype(jnp.float32)
     output = inputs + mixed + dense_shift + down_shift
-    again = (
-        lax.all_gather(w_qkv, ("fsdp", "ctx"), axis=0, tiled=True),
-        lax.all_gather(w_dense, ("fsdp", "ctx"), axis=1, tiled=True),
-        lax.all_gather(w_fc1, ("fsdp", "ctx"), axis=0, tiled=True),
-        lax.all_gather(w_fc2, ("fsdp", "ctx"), axis=1, tiled=True),
-    )
-    qkv_flat = again[0].reshape(model_width, 3 * local_cols)
-    dense_full, up_full, down_full = (again[1], again[2], again[3])
     grad_out = jnp.concatenate(
         [dy_prompt[0], dy_cont[0].reshape(cont_count * cont_len, model_width)], axis=0
     )
@@ -202,58 +187,82 @@
     )
     prompt_key_grads, prompt_value_grads = (
         lax.psum_scatter(
-            grad_keys[:prompt_len].reshape(prompt_len, local_cols),
+            grad_keys[:prompt_len].reshape(prompt_len, local_cols).astype(jnp.bfloat16),
             "ctx",
             scatter_dimension=0,
             tiled=True,
         ),
         lax.psum_scatter(
-            grad_values[:prompt_len].reshape(prompt_len, local_cols),
+            grad_values[:prompt_len].reshape(prompt_len, local_cols).astype(jnp.bfloat16),
             "ctx",
             scatter_dimension=0,
             tiled=True,
         ),
     )
     grad_keys = jnp.concatenate(
-        [prompt_key_grads.reshape(p_rows, head_count, HD), grad_keys[prompt_len:]], axis=0
+        [prompt_key_grads.reshape(p_rows, head_count, HD).astype(jnp.float32), grad_keys[prompt_len:]], axis=0
     )
     grad_values = jnp.concatenate(
-        [prompt_value_grads.reshape(p_rows, head_count, HD), grad_values[prompt_len:]], axis=0
+        [prompt_value_grads.reshape(p_rows, head_count, HD).astype(jnp.float32), grad_values[prompt_len:]], axis=0
     )
     grad_projected = jnp.stack(
         [rotate(grad_queries, cos_t, -sin_t), rotate(grad_keys, cos_t, -sin_t), grad_values], axis=1
     )
     grad_proj_low = grad_projected.reshape(row_count, 3 * local_cols).astype(jnp.bfloat16)
-    grad_qkv = jnp.dot(ln_one.T, grad_proj_low, preferred_element_type=jnp.float32).reshape(
-        model_width, 3, local_cols
-    )
-    grad_qkv_bias = jnp.sum(grad_proj_low.astype(jnp.float32), axis=0).reshape(3, local_cols)
+    moment_one = jnp.dot(unit_low.T, grad_proj_low, preferred_element_type=jnp.float32)
+    grad_qkv_bias = jnp.sum(grad_proj_low.astype(jnp.float32), axis=0)
     grad_norm_one = jnp.dot(grad_proj_low, qkv_flat.T, preferred_element_type=jnp.float32)
     grad_active = jnp.dot(grad_out, down_full.T, preferred_element_type=jnp.float32)
     gelu_back = jax.vjp(exact_gelu, hidden)[1]
     grad_hidden_low = gelu_back(grad_active)[0].astype(jnp.bfloat16)
-    grad_up = jnp.dot(ln_two.T, grad_hidden_low, preferred_element_type=jnp.float32)
+    moment_two = jnp.dot(unit_low.T, grad_hidden_low, preferred_element_type=jnp.float32)
     grad_up_bias = jnp.sum(grad_hidden_low.astype(jnp.float32), axis=0)
     grad_norm_two = jnp.dot(grad_hidden_low, up_full.T, preferred_element_type=jnp.float32)
-    norm_back = jax.vjp(norm_pair, inputs, gain_one, shift_one, gain_two, shift_two)[1]
-    full_one = lax.psum(grad_norm_one, "tp")
-    full_two = lax.psum(grad_norm_two, "tp")
-    grad_in, grad_gain_one, grad_shift_one, grad_gain_two, grad_shift_two = norm_back(
-        (full_one, full_two)
-    )
-    grad_inputs = grad_in + grad_out.astype(jnp.float32)
-    owned = (
-        lax.psum_scatter(grad_qkv, ("fsdp", "ctx"), scatter_dimension=0, tiled=True),
-        lax.psum_scatter(grad_dense, ("fsdp", "ctx"), scatter_dimension=1, tiled=True),
-        lax.psum_scatter(grad_up, ("fsdp", "ctx"), scatter_dimension=0, tiled=True),
-        lax.psum_scatter(grad_down, ("fsdp", "ctx"), scatter_dimension=1, tiled=True),
-        lax.psum_scatter(grad_shift, ("fsdp", "ctx"), scatter_dimension=0, tiled=True),
-        lax.psum_scatter(grad_gain_one, ("fsdp", "ctx"), scatter_dimension=0, tiled=True),
-        lax.psum_scatter(grad_shift_one, ("fsdp", "ctx"), scatter_dimension=0, tiled=True),
-        lax.psum_scatter(grad_gain_two, ("fsdp", "ctx"), scatter_dimension=0, tiled=True),
-        lax.psum_scatter(grad_shift_two, ("fsdp", "ctx"), scatter_dimension=0, tiled=True),
-    )
-    bias_qkv_total, bias_up_total = lax.psum((grad_qkv_bias, grad_up_bias), ("fsdp", "ctx"))
+    turned = (grad_norm_one * gain_one + grad_norm_two * gain_two).astype(jnp.bfloat16)
+    turned = lax.psum(turned, "tp").astype(jnp.float32)
+    grad_inputs = grad_out.astype(jnp.float32) + scale * (
+        turned
+        - jnp.mean(turned, axis=-1, keepdims=True)
+        - unit * jnp.mean(turned * unit, axis=-1, keepdims=True)
+    )
+    both = ("fsdp", "ctx")
+
+    def scatter(array, axis):
+        return lax.psum_scatter(
+            array.astype(jnp.bfloat16), both, scatter_dimension=axis, tiled=True
+        ).astype(jnp.float32)
+
+    own_one = scatter(moment_one, 0)
+    own_two = scatter(moment_two, 0)
+    d_dense = scatter(grad_dense, 1)
+    d_down = scatter(grad_down, 1)
+    bias_qkv_total, bias_up_total, shift_total = lax.psum(
+        (grad_qkv_bias, grad_up_bias, grad_shift), both
+    )
+    own_rows = w_qkv.shape[0]
+    own_place = (lax.axis_index("fsdp") * lax.axis_size("ctx") + piece_index) * own_rows
+    d_shift = lax.dynamic_slice_in_dim(shift_total, own_place, own_rows)
+    own_qkv = w_qkv.reshape(own_rows, 3 * local_cols).astype(jnp.float32)
+    own_up = w_fc1.astype(jnp.float32)
+    small = lax.psum(
+        jnp.stack(
+            [
+                jnp.sum(own_one * own_qkv, axis=1),
+                jnp.sum(own_qkv * bias_qkv_total, axis=1),
+                jnp.sum(own_two * own_up, axis=1),
+                jnp.sum(own_up * bias_up_total, axis=1),
+            ]
+        ),
+        "tp",
+    )
+    d_qkv = (
+        own_one * ln1_gain.astype(jnp.float32)[:, None]
+        + ln1_bias.astype(jnp.float32)[:, None] * bias_qkv_total
+    ).reshape(own_rows, 3, local_cols)
+    d_up = (
+        own_two * ln2_gain.astype(jnp.float32)[:, None]
+        + ln2_bias.astype(jnp.float32)[:, None] * bias_up_total
+    )
     y_prompt = output[:p_rows][None]
     y_cont = output[p_rows:].reshape(1, cont_count, cont_len, model_width)
     dx_prompt = grad_inputs[:p_rows][None]
@@ -263,18 +272,18 @@
         y_cont,
         dx_prompt,
         dx_cont,
-        owned[0],
-        bias_qkv_total,
-        owned[1],
-        owned[4],
-        owned[2],
+        d_qkv,
+        bias_qkv_total.reshape(3, local_cols),
+        d_dense,
+        d_shift,
+        d_up,
         bias_up_total,
-        owned[3],
-        owned[4],
-        owned[5],
-        owned[6],
-        owned[7],
-        owned[8],
+        d_down,
+        d_shift,
+        small[0],
+        small[1],
+        small[2],
+        small[3],
     )
 
 

time: 1050 us -> 642 us (0.61)
  waiting for transfers between devices: 609 us -> 209 us
  matrix products: 150 us -> 136 us
  blocking collectives: 159 us -> 170 us
    psum x2 -> x1, waiting for transfers between devices: 455 us -> 156 us  [on_device(): lax.psum((attn_part + mlp_part).astype(jnp.bfloat16), 'tp')]
    reduce_scatter x5 -> x3, waiting for transfers between devices: 148 us -> 36.1 us  [the longest x2 36 us: scatter(): lax.psum_scatter(array.astype(jnp.bfloat16), both, scatter_dimension=axis...]
    unnamed x11 -> x12, waiting for transfers between devices: 1.52 us -> 16.7 us
    psum x1 -> x2, blocking collectives: 26.6 us -> 38.6 us  [the longest x1 26.8 us: on_device(): lax.psum((grad_qkv_bias, grad_up_bias, grad_shift), both)]
  transfers between devices with their start and end apart: 11 -> 10, of which waited for: 6 -> 4; matrix products, arithmetic and copies ran while one was open for 23% -> 36% of each run, Pallas kernels for 0% -> 0%
where the time goes in v1:
time: 642 us; the launch traced here: 633 us
  waiting for transfers between devices  209 us (33%)
  blocking collectives  170 us (26%)
  matrix products  136 us (21%)
  other arithmetic  68.7 us (11%)
  local copies, waits for them, and re-layouts  32.7 us (5%)
  between operations  15.6 us (2%)
    psum x1, waiting for transfers between devices, on_device(): lax.psum((attn_part + mlp_part).astype(jnp.bfloat16), 'tp')  156 us
    reduce_scatter x2, waiting for transfers between devices, scatter(): lax.psum_scatter(array.astype(jnp.bfloat16), both, scatter_dimension=axis...  36 us
    psum x1, blocking collectives, on_device(): lax.psum((grad_qkv_bias, grad_up_bias, grad_shift), both)  26.8 us
    all_gather x1, blocking collectives, on_device(): lax.all_gather(w_dense, ('fsdp', 'ctx'), axis=1, tiled=True)  24.7 us
    convert_element_type x1, other arithmetic, on_device(): grad_scores = (probs * (grad_probs - inner)).astype(jnp.bfloat16)  24.7 us
    dot_general x1, matrix products, on_device(): jnp.einsum('qhd,khd->hqk', grad_attended, all_values, preferred_element_t...  22 us
    unnamed x12, waiting for transfers between devices  16.7 us
    unnamed x135, local copies, waits for them, and re-layouts  16.2 us
  transfers between devices with their start and end apart: 10, of which 4 were waited for; matrix products, arithmetic and copies ran while one was open for 36% of the time, Pallas kernels for 0%

profile of v1, /device:TPU:0, one launch (start us, length us, event | category | flops | bytes accessed | tf_op | source)
XLA Modules:
  0.0 633.0 jit_solution(4390822750926472987)
XLA Ops:
  14.6 14.7 %all-gather = bf16[8,1,128]{2,1,0:T(2,128)(2,1)S(1)} all-gather(bf16[1,1,128]{2,1,0:T(2,128)(2,1)S(1)} %bitcast.164), channel_id=1, replica_groups=mesh['fsdp'=2,'ctx'=4,'tp'=4] {'fsdp','ctx'}, dimensions={0}, use_global_device_ids=true | all-gather | bytes 2304 | tf_op jit(solution)/shard_map/all_gather | solution.py:75
  29.3 13.2 %all-gather.1 = bf16[8,1,128]{2,1,0:T(2,128)(2,1)S(1)} all-gather(bf16[1,1,128]{2,1,0:T(2,128)(2,1)S(1)} %bitcast.165), channel_id=1, replica_groups=mesh['fsdp'=2,'ctx'=4,'tp'=4] {'fsdp','ctx'}, dimensions={0}, use_global_device_ids=true | all-gather | bytes 2304 | tf_op jit(solution)/shard_map/all_gather | solution.py:76
  44.1 24.7 %all_gather.41 = bf16[256,1024]{1,0:T(8,128)(2,1)S(1)} all-gather(bf16[256,128]{1,0:T(8,128)(2,1)S(1)} %copy-done.30), channel_id=1, replica_groups=mesh['fsdp'=2,'ctx'=4,'tp'=4] {'fsdp','ctx'}, dimensions={1}, use_global_device_ids=true | all-gather | bytes 589824 | tf_op jit(solution)/shard_map/all_gather | solution.py:70
  68.9 13.9 %all-gather.2 = bf16[8,1,128]{2,1,0:T(2,128)(2,1)S(1)} all-gather(bf16[1,1,128]{2,1,0:T(2,128)(2,1)S(1)} %bitcast.162), channel_id=1, replica_groups=mesh['fsdp'=2,'ctx'=4,'tp'=4] {'fsdp','ctx'}, dimensions={0}, use_global_device_ids=true | all-gather | bytes 2304 | tf_op jit(solution)/shard_map/all_gather | solution.py:77
  83.9 13.2 %all-gather.3 = bf16[8,1,128]{2,1,0:T(2,128)(2,1)S(1)} all-gather(bf16[1,1,128]{2,1,0:T(2,128)(2,1)S(1)} %bitcast.163), channel_id=1, replica_groups=mesh['fsdp'=2,'ctx'=4,'tp'=4] {'fsdp','ctx'}, dimensions={0}, use_global_device_ids=true | all-gather | bytes 2304 | tf_op jit(solution)/shard_map/all_gather | solution.py:78
  108.2 13.2 %all_gather.40 = bf16[1024,256]{0,1:T(8,128)(2,1)S(1)} all-gather(bf16[256,256]{0,1:T(8,128)(2,1)S(1)} %bitcast.143), channel_id=1, replica_groups=mesh['fsdp'=2,'ctx'=4,'tp'=4] {'ctx'}, dimensions={0}, use_global_device_ids=true | all-gather | bytes 655360 | tf_op jit(solution)/shard_map/all_gather | solution.py:132
  121.4 12.8 %fusion = (f32[4,1024]{1,0:T(4,128)S(1)}, f32[4,1024,1792]{2,1,0:T(8,128)}) fusion(pred[1024,1792]{1,0:T(8,128)(4,1)S(1)} %fusion.2, bf16[1024,4,48]{0,2,1:T(8,128)(2,1)S(1)} %slice.242, bf16[1024,4,16]{0,2,1:T(8,128)(2,1)S(1)} %get-tuple-element.95, bf16[1024,4,64]{0,2,1:T(8,128)(2,1)S(1)} %bitcast.121, bf16[1024,4,48]{0,2,1:T(8,128)(2,1)S(1)} %slice.243, ...), kind=kOutput, calls=%fused_computation.5 | convolution fusion | flops 966717440 | bytes 32784384 | tf_op jit(solution)/shard_map/qhd,khd->hqk/dot_general | solution.py:39
  134.2 13.8 %exponential_reduce_fusion = f32[4,1024]{1,0:T(4,128)S(1)} fusion(f32[4,1024,1792]{2,1,0:T(8,128)} %get-tuple-element.107, f32[4,1024]{1,0:T(4,128)S(1)} %get-tuple-element.106, pred[1024,1792]{1,0:T(8,128)(4,1)S(1)} %fusion.2), kind=kLoop, calls=%fused_computation.3 | loop fusion | flops 29356032 | bytes 31227904 | tf_op jit(solution)/shard_map/reduce_sum | solution.py:145
  148.0 12.3 %all_gather.39 = bf16[1024,256]{0,1:T(8,128)(2,1)S(1)} all-gather(bf16[256,256]{0,1:T(8,128)(2,1)S(1)} %bitcast.144), channel_id=1, replica_groups=mesh['fsdp'=2,'ctx'=4,'tp'=4] {'ctx'}, dimensions={0}, use_global_device_ids=true | all-gather | bytes 655360 | tf_op jit(solution)/shard_map/all_gather | solution.py:133
  160.4 22.0 %multiply_reduce_fusion = (f32[4,1024]{1,0:T(4,128)S(1)}, f32[4,1024,1792]{2,1,0:T(8,128)}) fusion(f32[4,1024,1792]{2,1,0:T(8,128)} %get-tuple-element.107, f32[4,1024]{1,0:T(4,128)S(1)} %log_add_fusion, pred[1024,1792]{1,0:T(8,128)(4,1)S(1)} %fusion.2, bf16[1024,4,64]{0,2,1:T(8,128)(2,1)S(1)} %bitcast.135, bf16[768,4,64]{0,2,1:T(8,128)(2,1)S(1)} %slice_bitcast_fusion.4, ...), kind=kOutput, calls=%fused_computation.1 | convolution fusion | flops 978055168 | bytes 62029824 | tf_op jit(solution)/shard_map/qhd,khd->hqk/dot_general | solution.py:173
  182.4 24.7 %multiply_convert_fusion = bf16[4,1024,1792]{2,1,0:T(8,128)(2,1)} fusion(f32[4,1024,1792]{2,1,0:T(8,128)} %get-tuple-element.109, f32[4,1024,1792]{2,1,0:T(8,128)} %get-tuple-element.107, f32[4,1024]{1,0:T(4,128)S(1)} %get-tuple-element.108, f32[4,1024]{1,0:T(4,128)S(1)} %log_add_fusion, pred[1024,1792]{1,0:T(8,128)(4,1)S(1)} %fusion.2), kind=kLoop, calls=%fused_computation | loop fusion | flops 44040192 | bytes 75268096 | tf_op jit(solution)/shard_map/convert_element_type | solution.py:177
  207.1 7.8 %fusion.25 = f32[1792,4,64]{0,2,1:T(8,128)S(1)} fusion(bf16[4,1024,1792]{2,1,0:T(8,128)(2,1)} %multiply_convert_fusion, bf16[1024,4,48]{0,2,1:T(8,128)(2,1)S(1)} %slice.243, bf16[1024,4,16]{0,2,1:T(8,128)(2,1)S(1)} %get-tuple-element.96), kind=kOutput, calls=%fused_computation.57 | convolution fusion | flops 941031424 | bytes 17039360 | tf_op jit(solution)/shard_map/hqk,qhd->khd/dot_general | solution.py:183
  216.7 14.1 %convolution_convert_fusion.3 = bf16[4,64,1024]{2,1,0:T(8,128)(2,1)} fusion(bf16[768,4,64]{0,2,1:T(8,128)(2,1)} %copy-done.13, bf16[1024,4,64]{0,2,1:T(8,128)(2,1)} %bitcast.120, f32[4,1024,1792]{2,1,0:T(8,128)} %get-tuple-element.107, f32[4,1024]{1,0:T(4,128)S(1)} %log_add_fusion, pred[1024,1792]{1,0:T(8,128)(4,1)S(1)} %fusion.2), kind=kOutput, calls=%fused_computation.83 | convolution fusion | flops 970981376 | bytes 32653312 | tf_op jit(solution)/shard_map/hqk,khd->qhd/dot_general | solution.py:147
  231.1 13.7 %convolution_bitcast_fusion = bf16[1792,4,64]{0,2,1:T(8,128)(2,1)S(1)} fusion(bf16[1024,4,64]{0,2,1:T(8,128)(2,1)} %bitcast.134, f32[4,1024,1792]{2,1,0:T(8,128)} %get-tuple-element.107, f32[4,1024]{1,0:T(4,128)S(1)} %log_add_fusion, pred[1024,1792]{1,0:T(8,128)(4,1)S(1)} %fusion.2), kind=kOutput, calls=%fused_computation.56 | convolution fusion | flops 968884224 | bytes 32653312 | tf_op jit(solution)/shard_map/hqk,qhd->khd/dot_general | solution.py:185
  246.5 10.2 %fusion.43 = f32[1024,4,64]{0,2,1:T(8,128)S(1)} fusion(bf16[4,1024,1792]{2,1,0:T(8,128)(2,1)} %multiply_convert_fusion, bf16[1024,4,48]{0,2,1:T(8,128)(2,1)} %copy-done.6, bf16[1024,4,16]{0,2,1:T(8,128)(2,1)S(1)} %get-tuple-element.95, bf16[1024,4,64]{0,2,1:T(8,128)(2,1)} %bitcast.122), kind=kOutput, calls=%fused_computation.82 | convolution fusion | flops 943915008 | bytes 16777216 | tf_op jit(solution)/shard_map/hqk,khd->qhd/dot_general | solution.py:179
  263.9 16.0 %multiply_convert_fusion.1 = (bf16[1024,1024]{1,0:T(8,128)(2,1)S(1)}, f32[1024,1024]{1,0:T(8,128)}, f32[1024,1024]{1,0:T(8,128)}) fusion(f32[1024]{0:T(1024)S(1)} %copy-done.37, bf16[1024,1024]{1,0:T(8,128)(2,1)} %all-gather.12.cloned.1.call-done, f32[1024]{0:T(1024)S(1)} %bitcast.155, f32[1024]{0:T(1024)S(1)} %bitcast.153, f32[1024]{0:T(1024)S(1)} %copy-done.34, ...), kind=kOutput, calls=%fused_computation.39 | convolution fusion | flops 2226126848 | bytes 14700544 | tf_op jit(solution)/shard_map/dot_general | solution.py:150
  318.7 12.4 %all-gather.4 = bf16[8,1,128]{2,1,0:T(2,128)(2,1)S(1)} all-gather(bf16[1,1,128]{2,1,0:T(2,128)(2,1)S(1)} %bitcast.166), channel_id=1, replica_groups=mesh['fsdp'=2,'ctx'=4,'tp'=4] {'fsdp','ctx'}, dimensions={0}, use_global_device_ids=true | all-gather | bytes 2304 | tf_op jit(solution)/shard_map/all_gather | solution.py:73
  331.1 13.5 %all-gather.5 = bf16[8,1,128]{2,1,0:T(2,128)(2,1)S(1)} all-gather(bf16[1,1,128]{2,1,0:T(2,128)(2,1)S(1)} %bitcast.167), channel_id=1, replica_groups=mesh['fsdp'=2,'ctx'=4,'tp'=4] {'fsdp','ctx'}, dimensions={0}, use_global_device_ids=true | all-gather | bytes 2304 | tf_op jit(solution)/shard_map/all_gather | solution.py:74
  351.3 15.2 %reduce-scatter.21.cloned.1.call-done = bf16[128,1024]{1,0:T(8,128)(2,1)} async-done(((bf16[1024,1024]{1,0:T(8,128)(2,1)}), bf16[128,1024]{1,0:T(8,128)(2,1)}) %reduce-scatter.21.cloned.1.call-update) | async-done | bytes 262160
  368.4 156.4 %all-reduce.8.cloned.1.call-done = (bf16[1024,1024]{1,0:T(8,128)(2,1)}, bf16[1024,1024]{1,0:T(8,128)(2,1)}) async-done(((bf16[1024,1024]{1,0:T(8,128)(2,1)}, bf16[1024,1024]{1,0:T(8,128)(2,1)}), (bf16[1024,1024]{1,0:T(8,128)(2,1)}, bf16[1024,1024]{1,0:T(8,128)(2,1)})) %all-reduce.8.cloned.1.call-update) | async-done | bytes 4194320 | tf_op jit(solution)/shard_map/psum | solution.py:155
  528.6 6.2 convert_reduce_fusion.2
  534.8 26.8 %all-reduce.4 = (f32[768]{0:T(1024)S(1)}, f32[1024]{0:T(1024)S(1)}, f32[1024]{0:T(1024)S(1)}) all-reduce(f32[768]{0:T(1024)S(1)} %reduce_sum.126, f32[1024]{0:T(1024)S(1)} %get-tuple-element.79, f32[1024]{0:T(1024)S(1)} %get-tuple-element.110), channel_id=1, replica_groups=mesh['fsdp'=2,'ctx'=4,'tp'=4] {'fsdp','ctx'}, use_global_device_ids=true, to_apply=%region_13.14 | all-reduce | flops 2816 | bytes 22528 | tf_op jit(solution)/shard_map/psum | solution.py:239
  575.7 35.0 %reduce-scatter.15.cloned.1.call-done = bf16[128,768]{1,0:T(8,128)(2,1)} async-done(((bf16[1024,768]{1,0:T(8,128)(2,1)}), bf16[128,768]{1,0:T(8,128)(2,1)}) %reduce-scatter.15.cloned.1.call-update) | async-done | bytes 196624 | tf_op jit(solution)/shard_map/reduce_scatter | solution.py:231
  611.8 11.7 %psum.47 = f32[4,128]{1,0:T(4,128)S(1)} all-reduce(f32[4,128]{1,0:T(4,128)S(1)} %pad_maximum_fusion.11), channel_id=1, replica_groups=mesh['fsdp'=2,'ctx'=4,'tp'=4] {'tp'}, use_global_device_ids=true, to_apply=%region_25.26 | all-reduce | flops 512 | bytes 4096 | tf_op jit(solution)/shard_map/psum | solution.py:247
  (251 shorter events, 99.9 us)
Async XLA Ops:
  7.2 35.3 %copy-start.43 = (bf16[3,256]{1,0:T(4,128)(2,1)S(1)}, bf16[3,256]{1,0:T(4,128)(2,1)}, u32[]{:S(2)}) copy-start(bf16[3,256]{1,0:T(4,128)(2,1)} %param.21) | copy-start | bytes 4612
  7.2 35.3 %copy-start.45 = (s32[1,3]{1,0:T(1,128)S(1)}, s32[1,3]{1,0:T(1,128)}, u32[]{:S(2)}) copy-start(s32[1,3]{1,0:T(1,128)} %param.19) | copy-start | bytes 40
  7.2 36.9 %copy-start.30 = (bf16[256,128]{1,0:T(8,128)(2,1)S(1)}, bf16[256,128]{1,0:T(8,128)(2,1)}, u32[]{:S(2)}) copy-start(bf16[256,128]{1,0:T(8,128)(2,1)} %param.22) | copy-start | bytes 196612
  7.2 61.6 %copy-start.46 = (bf16[128]{0:T(256)(128)(2,1)S(1)}, bf16[128]{0:T(256)(128)(2,1)}, u32[]{:S(2)}) copy-start(bf16[128]{0:T(256)(128)(2,1)} %param.30) | copy-start | bytes 772
  7.3 76.0 %copy-start.44 = (bf16[1024]{0:T(1024)(128)(2,1)S(1)}, bf16[1024]{0:T(1024)(128)(2,1)}, u32[]{:S(2)}) copy-start(bf16[1024]{0:T(1024)(128)(2,1)} %param.25) | copy-start | bytes 6148
  7.3 76.6 %copy-start.48 = (bf16[128]{0:T(256)(128)(2,1)S(1)}, bf16[128]{0:T(256)(128)(2,1)}, u32[]{:S(2)}) copy-start(bf16[128]{0:T(256)(128)(2,1)} %param.31) | copy-start | bytes 772
  7.3 90.5 %copy-start.14 = (bf16[1,3,256,1024]{3,2,1,0:T(8,128)(2,1)S(1)}, bf16[1,3,256,1024]{3,2,1,0:T(8,128)(2,1)}, u32[]{:S(2)}) copy-start(bf16[1,3,256,1024]{3,2,1,0:T(8,128)(2,1)} %param.33) | copy-start | bytes 4718596
  7.3 96.0 %all-gather.10.cloned.1.call-start = ((), (), s32[]{:S(2)}) async-start(), calls=%async_computation.6 | async-start | bytes 1769472 | tf_op jit(solution)/shard_map/all_gather | solution.py:69
  9.3 254.5 %all-gather.12.cloned.1.call-start = ((), (), s32[]{:S(2)}) async-start(), calls=%async_computation.7 | async-start | bytes 2359296 | tf_op jit(solution)/shard_map/all_gather | solution.py:71
  10.0 279.2 %all-gather.14.cloned.1.call-start = ((), (), s32[]{:S(2)}) async-start(), calls=%async_computation.8 | async-start | bytes 2359296 | tf_op jit(solution)/shard_map/all_gather | solution.py:72
  10.8 291.5 %reduce-scatter.11.cloned.1.call-start = ((), (), s32[]{:S(2)}) async-start(), calls=%async_computation.9 | async-start | bytes 655360 | tf_op jit(solution)/shard_map/reduce_scatter | solution.py:189
  12.8 90.5 %copy-start.31 = (f32[1024]{0:T(1024)}, f32[1024]{0:T(1024)S(1)}, u32[]{:S(2)}) copy-start(f32[1024]{0:T(1024)S(1)} %broadcast_multiply_fusion.2) | copy-start | bytes 12292
  14.6 88.8 %copy-start.33 = (f32[1024]{0:T(1024)}, f32[1024]{0:T(1024)S(1)}, u32[]{:S(2)}) copy-start(f32[1024]{0:T(1024)S(1)} %add_rsqrt_fusion) | copy-start | bytes 12292
  29.3 74.1 %copy-start.38 = (f32[8,1,128]{2,1,0:T(1,128)}, f32[8,1,128]{2,1,0:T(1,128)S(1)}, u32[]{:S(2)}) copy-start(f32[8,1,128]{2,1,0:T(1,128)S(1)} %convert_element_type.249) | copy-start | bytes 12292
  68.9 28.9 %copy-start.9 = (bf16[256,1024]{1,0:T(8,128)(2,1)}, bf16[256,1024]{1,0:T(8,128)(2,1)S(1)}, u32[]{:S(2)}) copy-start(bf16[256,1024]{1,0:T(8,128)(2,1)S(1)} %all_gather.41) | copy-start | bytes 1572868
  107.7 52.6 %copy-start.13 = (bf16[768,4,64]{0,2,1:T(8,128)(2,1)}, bf16[768,4,64]{0,2,1:T(8,128)(2,1)S(1)}, u32[]{:S(2)}) copy-start(bf16[768,4,64]{0,2,1:T(8,128)(2,1)S(1)} %slice_bitcast_fusion.4) | copy-start | bytes 1179652
  134.2 26.1 %copy-start.23 = (bf16[1024,256]{0,1:T(8,128)(2,1)S(1)}, bf16[1024,256]{0,1:T(8,128)(2,1)}, u32[]{:S(2)}) copy-start(bf16[1024,256]{0,1:T(8,128)(2,1)} %convolution_convert_fusion.5) | copy-start | bytes 1572868
  230.9 73.6 %reduce-scatter.13.cloned.1.call-start = ((), (), s32[]{:S(2)}) async-start(), calls=%async_computation.10 | async-start | bytes 655360 | tf_op jit(solution)/shard_map/reduce_scatter | solution.py:195
  246.4 98.4 %reduce-scatter.19.cloned.1.call-start = ((), (), s32[]{:S(2)}) async-start(), calls=%async_computation.13 | async-start | bytes 589824
  263.7 102.8 %reduce-scatter.21.cloned.1.call-start = ((), (), s32[]{:S(2)}) async-start(), calls=%async_computation.14 | async-start | bytes 2359296
  288.9 235.9 %all-reduce.8.cloned.1.call-start = ((), (), s32[]{:S(2)}) async-start(), calls=%async_computation.15 | async-start | bytes 8388608 | tf_op jit(solution)/shard_map/psum | solution.py:155
  312.7 31.9 %copy-start.7 = (bf16[128,3,256]{0,2,1:T(8,128)(2,1)S(1)}, bf16[128,3,256]{0,2,1:T(8,128)(2,1)}, u32[]{:S(2)}) copy-start(bf16[128,3,256]{0,2,1:T(8,128)(2,1)} %copy.40) | copy-start | bytes 589828
  312.7 256.3 %reduce-scatter.17.cloned.1.call-start = ((), (), s32[]{:S(2)}) async-start(), calls=%async_computation.12 | async-start | bytes 2359296 | tf_op jit(solution)/shard_map/reduce_scatter | solution.py:231
  318.6 292.1 %reduce-scatter.15.cloned.1.call-start = ((), (), s32[]{:S(2)}) async-start(), calls=%async_computation.11 | async-start | bytes 1769472 | tf_op jit(solution)/shard_map/reduce_scatter | solution.py:231
  (50 other events, 321.6 us)
Sparse Core Ops, SparseCore 0:
  10.0 28.5 all-gather.9
  40.5 32.9 all-gather.11
  75.4 27.9 all-gather.13
  231.0 25.1 reduce-scatter.10
  259.7 24.7 reduce-scatter.12
  287.4 34.1 reduce-scatter.18
  325.2 41.2 reduce-scatter.20
  369.5 155.3 all-reduce.7
  528.5 40.5 reduce-scatter.16
  572.2 38.4 reduce-scatter.14

commit v2 on v0

v2 whole, which is shorter than its diff:
```python
import functools

import jax
import jax.numpy as jnp
import numpy as np
from jax import lax
from jax.experimental import pallas as pl
from jax.experimental.pallas import tpu as pltpu
from jax.sharding import PartitionSpec as P

HD = 64
ROT = 16
EPS = 1e-05
MASKED = -1e30
F32 = jnp.float32
BF16 = jnp.bfloat16
MESH = pl.DeviceIdType.MESH
CHUNK = 128
ERF = (0.254829592, -0.284496736, 1.421413741, -1.453152027, 1.061405429)


def nn(left, right):
    return jnp.dot(left, right, preferred_element_type=F32)


def nt(left, right):
    return lax.dot_general(left, right, (((1,), (1,)), ((), ())), preferred_element_type=F32)


def remote(src, dst, send_sem, recv_sem, device):
    return pltpu.make_async_remote_copy(
        src_ref=src,
        dst_ref=dst,
        send_sem=send_sem,
        recv_sem=recv_sem,
        device_id=device,
        device_id_type=MESH,
    )


def turn(values, cos_t, sin_t):
    lane = lax.broadcasted_iota(jnp.int32, cos_t.shape, 1)
    low_half = lax.rem(lane, HD) < ROT // 2
    pieces = []
    for start in range(0, values.shape[1], 128):
        piece = values[:, start : start + 128]
        up = pltpu.roll(piece, 128 - ROT // 2, 1)
        down = pltpu.roll(piece, ROT // 2, 1)
        pieces.append(piece * cos_t + jnp.where(low_half, up, down) * sin_t)
    return jnp.concatenate(pieces, axis=1) if len(pieces) > 1 else pieces[0]


def layer_kernel(sizes, *refs):
    nf, nc, nt_axis = sizes["nf"], sizes["nc"], sizes["tp"]
    own, cols, ff, width = sizes["own"], sizes["cols"], sizes["ff"], sizes["width"]
    length, slots, total = sizes["length"], sizes["slots"], sizes["total"]
    part, pieces_one, pieces_two = sizes["part"], sizes["pieces_one"], sizes["pieces_two"]
    (
        starts, freq, x_prompt, x_cont, dy_prompt, dy_cont, w_q, w_d, w_u, w_o,
        small, bias_q, bias_u,
        y_out, u_out, dw_out, sums_out, norms_out, small_out,
        xv, dyv, n_t, dy_t, wall, wsh, wd_tmp, wo_tmp, mean_s, scale_s, cos_s, sin_s,
        smallg, qb, kvb, kvp, k_t, v_t, ko_t, vo_t, qm, gm, o_t, dq_t, p_own, ds_own,
        ga, oa, gd, acc, kv_send, kv_recv,
        yb, ya, yt, ub, ua, ut, half_send, half_recv, piece_recv, dw_acc,
        sum_own, sum_f, sum_c, norm_own, norm_in,
        in_sem, small_sem, ws, wr, fs, fr, ls, kvs, kvr, gks, gkr,
        zs, za, zbs, zb, zo, hs, hr, ps, pr, ss, sr, ns, nr, os,
    ) = refs
    f, c, t = lax.axis_index("fsdp"), lax.axis_index("ctx"), lax.axis_index("tp")
    heads = cols // HD
    rows_all = slots * length
    prompt = nc * length
    first = 3 * cols
    edge = first + ff
    shard = f * nc + c
    own_rows = pl.ds(pl.multiple_of(shard * own, own), own)

    def ctx_to(step):
        return (f, lax.rem(c + step, nc), t)

    def ctx_from(step):
        return lax.rem(c + nc - step, nc)

    def mate_to(step):
        return (lax.rem(f + step, nf), c, t)

    def mate_from(step):
        return lax.rem(f + nf - step, nf)

    def tp_to(step):
        return (f, c, lax.rem(t + step, nt_axis))

    upper = lax.div(t, nt_axis // 2)
    inward = (f, c, t + 1 - 2 * upper)
    outward = (f, c, lax.rem(t - 1 + 2 * upper + nt_axis, nt_axis))
    at_end = (t == 0) | (t == nt_axis - 1)
    not_end = (t != 0) & (t != nt_axis - 1)
    in_middle = (t == nt_axis // 2 - 1) | (t == nt_axis // 2)
    not_middle = (t != nt_axis // 2 - 1) & (t != nt_axis // 2)

    loads = [
        (x_prompt, xv.at[pl.ds(0, length)]),
        (x_cont, xv.at[pl.ds(length, rows_all - length)]),
        (dy_prompt, dyv.at[pl.ds(0, length)]),
        (dy_cont, dyv.at[pl.ds(length, rows_all - length)]),
        (w_q.at[0], wsh.at[:, pl.ds(0, cols)]),
        (w_q.at[1], wsh.at[:, pl.ds(cols, cols)]),
        (w_q.at[2], wsh.at[:, pl.ds(2 * cols, cols)]),
        (w_u, wsh.at[:, pl.ds(first, ff)]),
    ]
    turned_in = sizes["turned"]
    if turned_in:
        loads += [(w_d, wsh.at[:, pl.ds(edge, cols)]), (w_o, wsh.at[:, pl.ds(edge + cols, ff)])]
    else:
        loads += [(w_d, wd_tmp), (w_o, wo_tmp)]
    loads = [pltpu.make_async_copy(src, dst, in_sem.at[i]) for i, (src, dst) in enumerate(loads)]
    for i in (4, 5, 6, 0, 1, 8, 7, 9, 2, 3):
        loads[i].start()

    barrier = pltpu.get_barrier_semaphore()
    greeted = [ctx_to(k) for k in range(1, nc)]
    greeted += [mate_to(g) for g in range(1, nf)]
    greeted += [tp_to(k) for k in range(1, nt_axis)]
    for device in greeted:
        pl.semaphore_signal(barrier, inc=1, device_id=device, device_id_type=MESH)
    pl.semaphore_wait(barrier, len(greeted))

    spans = (
        (0, first),
        (edge, cols),
        (first, ff),
        (edge + cols, ff),
    )

    def gather_copy(p, step, g):
        lanes = pl.ds(spans[p][0], spans[p][1])
        if g == 0:
            return remote(
                wsh.at[:, lanes],
                wall.at[own_rows, lanes],
                ws.at[p, step - 1],
                wr.at[p, step - 1],
                ctx_to(step),
            )
        held = f * nc + ctx_from(step)
        rows = pl.ds(pl.multiple_of(held * own, own), own)
        src = wsh.at[:, lanes] if step == 0 else wall.at[rows, lanes]
        return remote(
            src, wall.at[rows, lanes], fs.at[p, step, g - 1], fr.at[p, step, g - 1], mate_to(g)
        )

    def gather_local(p):
        lanes = pl.ds(spans[p][0], spans[p][1])
        return pltpu.make_async_copy(wsh.at[:, lanes], wall.at[own_rows, lanes], ls.at[p])

    def gather_start(p):
        for step in range(1, nc):
            gather_copy(p, step, 0).start()
        for g in range(1, nf):
            gather_copy(p, 0, g).start()
        gather_local(p).start()

    def gather_pass(p):
        for step in range(1, nc):
            gather_copy(p, step, 0).wait_recv()
            for g in range(1, nf):
                gather_copy(p, step, g).start()

    def gather_finish(p):
        gather_local(p).wait()
        for step in range(nc):
            for g in range(1, nf):
                gather_copy(p, step, g).wait_recv()

    def gather_sent(p):
        for step in range(1, nc):
            gather_copy(p, step, 0).wait_send()
        for step in range(nc):
            for g in range(1, nf):
                gather_copy(p, step, g).wait_send()

    def small_copy(step, g):
        if g == 0:
            return remote(
                small, smallg.at[shard], small_sem.at[0, step, 0], small_sem.at[1, step, 0], ctx_to(step)
            )
        held = f * nc + ctx_from(step)
        src = small if step == 0 else smallg.at[held]
        return remote(
            src, smallg.at[held], small_sem.at[0, step, g], small_sem.at[1, step, g], mate_to(g)
        )

    for step in range(1, nc):
        small_copy(step, 0).start()
    for g in range(1, nf):
        small_copy(0, g).start()
    for i in (4, 5, 6):
        loads[i].wait()
    gather_start(0)
    if not turned_in:
        loads[8].wait()
        wsh[:, edge : edge + cols] = wd_tmp[...].astype(F32).T.astype(BF16)
    else:
        loads[8].wait()
    gather_start(1)
    smallg[shard] = small[...]

    loads[0].wait()
    loads[1].wait()

    def statistics(slot, carry):
        rows = pl.ds(pl.multiple_of(slot * length, length), length)
        block = xv[rows, :].astype(F32)
        mean = jnp.mean(block, axis=1, keepdims=True)
        block = block - mean
        scale = lax.rsqrt(jnp.mean(block * block, axis=1, keepdims=True) + EPS)
        mean_s[rows, :] = mean
        scale_s[rows, :] = scale
        n_t[:, rows] = (block * scale).T.astype(BF16)
        before = starts[0, jnp.maximum(slot - 1, 0)]
        base = jnp.where(slot == 0, c * length, before)
        place = base + lax.broadcasted_iota(jnp.int32, (length, 128), 0)
        phase = place.astype(F32) * freq[0:1, :]
        cos_s[rows, :] = jnp.cos(phase)
        sin_s[rows, :] = jnp.sin(phase) * freq[1:2, :]
        return carry

    lax.fori_loop(0, slots, statistics, 0)

    for step in range(1, nc):
        small_copy(step, 0).wait_recv()
        for g in range(1, nf):
            small_copy(step, g).start()
    for step in range(nc):
        for g in range(1, nf):
            small_copy(step, g).wait_recv()
    parts = [smallg[i] for i in range(nf * nc)]
    whole = jnp.concatenate(parts, axis=1)
    small_out[...] = whole
    gain_one, shift_one = small_out[2:3, :], small_out[3:4, :]
    gain_two, shift_two = small_out[4:5, :], small_out[5:6, :]

    def normed(rows, gain, shift):
        block = (xv[rows, :].astype(F32) - mean_s[rows, :]) * scale_s[rows, :]
        return (block * gain + shift).astype(BF16)

    gather_pass(0)
    gather_finish(0)

    def project(slot):
        rows = pl.ds(pl.multiple_of(slot * length, length), length)
        both = nn(normed(rows, gain_one, shift_one), wall[:, 0:first])
        cos_t, sin_t = cos_s[rows, :], sin_s[rows, :]
        query = both[:, 0:cols] + bias_q[0:1, :].astype(F32)
        key = both[:, cols : 2 * cols] + bias_q[1:2, :].astype(F32)
        value = both[:, 2 * cols : first] + bias_q[2:3, :].astype(F32)
        qb[rows, :] = (turn(query, cos_t, sin_t) * 0.125).astype(BF16)
        kvb[rows, 0:cols] = turn(key, cos_t, sin_t).astype(BF16)
        kvb[rows, cols : 2 * cols] = value.astype(BF16)

    project(0)
    mine = pl.ds(pl.multiple_of(c * length, length), length)
    kvp[mine, :] = kvb[0:length, :]

    def kv_copy(step):
        return remote(
            kvb.at[pl.ds(0, length)], kvp.at[mine], kvs.at[step - 1], kvr.at[step - 1], ctx_to(step)
        )

    for step in range(1, nc):
        kv_copy(step).start()
    loads[7].wait()
    gather_start(2)
    loads[9].wait()
    if not turned_in:
        wsh[:, edge + cols : total] = wo_tmp[...].astype(F32).T.astype(BF16)
    gather_start(3)

    lax.fori_loop(1, slots, lambda slot, carry: (project(slot), carry)[1], 0)

    gather_pass(1)
    gather_finish(1)
    loads[2].wait()
    loads[3].wait()

    def back_dense(slot, carry):
        rows = pl.ds(pl.multiple_of(slot * length, length), length)
        block = dyv[rows, :]
        ga[rows, :] = nn(block, wall[:, edge : edge + cols]).astype(BF16)
        dy_t[:, rows] = block.astype(F32).T.astype(BF16)
        return carry

    lax.fori_loop(0, slots, back_dense, 0)

    for step in range(1, nc):
        kv_copy(step).wait_recv()
    k_t[...] = kvp[:, 0:cols].astype(F32).T.astype(BF16)
    v_t[...] = kvp[:, cols : 2 * cols].astype(F32).T.astype(BF16)

    def attend(slot, is_prompt):
        rows = pl.ds(pl.multiple_of(slot * length, length), length)
        head_of = lax.div(lax.broadcasted_iota(jnp.int32, (length, cols), 1), HD)
        query, grad = qb[rows, :], ga[rows, :]
        zero = jnp.zeros_like(query)
        for h in range(heads):
            qm[h * length : (h + 1) * length, :] = jnp.where(head_of == h, query, zero)
            gm[h * length : (h + 1) * length, :] = jnp.where(head_of == h, grad, zero)
        if not is_prompt:
            ko_t[...] = kvb[rows, 0:cols].astype(F32).T.astype(BF16)
            vo_t[...] = kvb[rows, cols : 2 * cols].astype(F32).T.astype(BF16)
            limit = starts[0, slot - 1]

        def one_head(h, carry):
            lanes = pl.ds(pl.multiple_of(h * length, length), length)
            lines = pl.ds(pl.multiple_of(h * HD, HD), HD)
            q_h, g_h = qm[lanes, :], gm[lanes, :]
            scores = nt(kvp[:, 0:cols], q_h)
            key_at = lax.broadcasted_iota(jnp.int32, scores.shape, 0)
            query_at = lax.broadcasted_iota(jnp.int32, scores.shape, 1)
            if is_prompt:
                seen = key_at <= query_at + c * length
            else:
                seen = key_at < limit
            scores = jnp.where(seen, scores, MASKED)
            highest = jnp.max(scores, axis=0, keepdims=True)
            if not is_prompt:
                scores_own = nt(kvb[rows, 0:cols], q_h)
                own_key = lax.broadcasted_iota(jnp.int32, scores_own.shape, 0)
                own_query = lax.broadcasted_iota(jnp.int32, scores_own.shape, 1)
                scores_own = jnp.where(own_key <= own_query, scores_own, MASKED)
                highest = jnp.maximum(highest, jnp.max(scores_own, axis=0, keepdims=True))
            probs = jnp.exp(scores - highest)
            norm = jnp.sum(probs, axis=0, keepdims=True)
            if not is_prompt:
                probs_own = jnp.exp(scores_own - highest)
                norm = norm + jnp.sum(probs_own, axis=0, keepdims=True)
            share = 1.0 / norm
            probs = probs * share
            probs_low = probs.astype(BF16)
            yb[0:prompt, lanes] = probs_low
            grads = nt(kvp[:, cols : 2 * cols], g_h)
            inner = jnp.sum(probs * grads, axis=0, keepdims=True)
            if not is_prompt:
                probs_own = probs_own * share
                own_low = probs_own.astype(BF16)
                p_own[:, lanes] = own_low
                grads_own = nt(kvb[rows, cols : 2 * cols], g_h)
                inner = inner + jnp.sum(probs_own * grads_own, axis=0, keepdims=True)
            back_low = (probs * (grads - inner)).astype(BF16)
            ub[0:prompt, lanes] = back_low
            out_t = nn(v_t[lines, :], probs_low)
            back_q = nn(k_t[lines, :], back_low)
            if not is_prompt:
                back_own = (probs_own * (grads_own - inner)).astype(BF16)
                ds_own[:, lanes] = back_own
                out_t = out_t + nn(vo_t[lines, :], own_low)
                back_q = back_q + nn(ko_t[lines, :], back_own)
            o_t[lines, :] = out_t
            dq_t[lines, :] = back_q
            return carry

        lax.fori_loop(0, heads, one_head, 0)
        cos_t, sin_t = cos_s[rows, :], -sin_s[rows, :]
        oa[rows, 0:cols] = o_t[...].T.astype(BF16)
        gd[rows, 0:cols] = turn(dq_t[...].T * 0.125, cos_t, sin_t).astype(BF16)
        stacked = heads * length
        back_k = nn(ub[0:prompt, 0:stacked], qm[...])
        back_v = nn(yb[0:prompt, 0:stacked], gm[...])
        if is_prompt:
            acc[:, 0:cols] = back_k
            acc[:, cols : 2 * cols] = back_v
        else:
            acc[:, 0:cols] += back_k
            acc[:, cols : 2 * cols] += back_v
            gd[rows, cols : 2 * cols] = turn(nn(ds_own[...], qm[...]), cos_t, sin_t).astype(BF16)
            gd[rows, 2 * cols : first] = nn(p_own[...], gm[...]).astype(BF16)

    attend(0, True)
    lax.fori_loop(1, slots, lambda slot, carry: (attend(slot, False), carry)[1], 0)

    def back_kv_copy(step):
        return remote(
            kv_send.at[step - 1], kv_recv.at[step - 1], gks.at[step - 1], gkr.at[step - 1], ctx_to(step)
        )

    for step in range(1, nc):
        there = pl.ds(pl.multiple_of(lax.rem(c + step, nc) * length, length), length)
        kv_send[step - 1] = acc[there, :].astype(BF16)
        back_kv_copy(step).start()

    chunks = rows_all // CHUNK
    sums = ((yb, ya, yt, y_out), (ub, ua, ut, u_out))

    def line(which, i):
        return sums[which], pl.ds(pl.multiple_of(i * CHUNK, CHUNK), CHUNK)

    def line_out(which, i, middle):
        (mine_ref, from_out, from_in, _), rows = line(which, i)
        target = from_in if middle else from_out
        landed = zb if middle else za
        return remote(
            mine_ref.at[rows], target.at[rows], zs.at[which, i], landed.at[which, i], inward
        )

    def line_home(which, i, middle):
        (_, from_out, from_in, _), rows = line(which, i)
        src = from_out if middle else from_in
        return remote(
            src.at[rows], from_in.at[rows], zbs.at[which, i], zb.at[which, i], outward
        )

    def line_store(which, i, middle):
        (_, from_out, from_in, out), rows = line(which, i)
        src = from_out if middle else from_in
        return pltpu.make_async_copy(src.at[rows], out.at[rows], zo.at[which, i])

    def line_send(which, i):
        @pl.when(in_middle)
        def _():
            line_out(which, i, True).start()

        @pl.when(not_middle)
        def _():
            line_out(which, i, False).start()

    def line_first(which, i):
        @pl.when(at_end)
        def _():
            line_send(which, i)

    def line_add(which, i):
        (mine_ref, from_out, _, _), rows = line(which, i)

        @pl.when(not_end)
        def _():
            line_out(which, i, False).wait_recv()
            mine_ref[rows, :] = (
                mine_ref[rows, :].astype(F32) + from_out[rows, :].astype(F32)
            ).astype(BF16)
            line_send(which, i)

    def line_back(which, i):
        (mine_ref, from_out, from_in, _), rows = line(which, i)

        @pl.when(in_middle)
        def _():
            line_out(which, i, True).wait_recv()
            from_out[rows, :] = (
                mine_ref[rows, :].astype(F32) + from_in[rows, :].astype(F32)
            ).astype(BF16)

            @pl.when(not_end)
            def _():
                line_home(which, i, True).start()

            line_store(which, i, True).start()

        @pl.when(not_middle)
        def _():
            line_home(which, i, False).wait_recv()

            @pl.when(not_end)
            def _():
                line_home(which, i, False).start()

            line_store(which, i, False).start()

    def line_done(which, i):
        line_out(which, i, True).wait_send()
        line_store(which, i, True).wait()

        @pl.when(not_end)
        def _():
            line_home(which, i, True).wait_send()

    for p in (2, 3):
        gather_pass(p)
    for p in (2, 3):
        gather_finish(p)

    def feed(slot, carry):
        rows = pl.ds(pl.multiple_of(slot * length, length), length)
        hidden = nn(normed(rows, gain_two, shift_two), wall[:, first:edge]) + bias_u[...].astype(F32)
        depth = jnp.abs(hidden) * np.float32(0.5**0.5)
        step = 1.0 / (1.0 + np.float32(0.3275911) * depth)
        poly = np.float32(ERF[4])
        for factor in ERF[3::-1]:
            poly = poly * step + np.float32(factor)
        bell = jnp.exp(-(depth * depth))
        tail = 0.5 * (poly * step) * bell
        below = jnp.where(hidden >= 0.0, 1.0 - tail, tail)
        oa[rows, cols : cols + ff] = (hidden * below).astype(BF16)
        slope = below + hidden * (bell * np.float32((2.0 * np.pi) ** -0.5))
        back = nn(dyv[rows, :], wall[:, edge + cols : total])
        gd[rows, first:edge] = (back * slope).astype(BF16)
        yb[rows, :] = nt(oa[rows, :], wall[:, edge:total]).astype(BF16)
        for i in range(length // CHUNK):
            line_first(0, slot * (length // CHUNK) + i)
        return carry

    lax.fori_loop(0, slots, feed, 0)

    grad_kv = acc[mine, :]
    for step in range(1, nc):
        back_kv_copy(step).wait_recv()
        grad_kv = grad_kv + kv_recv[step - 1].astype(F32)
    gd[0:length, cols : 2 * cols] = turn(
        grad_kv[:, 0:cols], cos_s[0:length, :], -sin_s[0:length, :]
    ).astype(BF16)
    gd[0:length, 2 * cols : first] = grad_kv[:, cols : 2 * cols].astype(BF16)

    def back_norms(slot, carry):
        rows = pl.ds(pl.multiple_of(slot * length, length), length)
        toward_x = nt(gd[rows, 0:first], wall[:, 0:first]) * gain_one
        toward_x = toward_x + nt(gd[rows, first:edge], wall[:, first:edge]) * gain_two
        ub[rows, :] = toward_x.astype(BF16)
        for i in range(length // CHUNK):
            line_first(1, slot * (length // CHUNK) + i)
        line_add(0, slot)
        return carry

    lax.fori_loop(0, slots, back_norms, 0)

    ones = jnp.ones((16, rows_all), BF16)
    sum_own[:, 0:edge] = nn(ones, gd[...])[0:8, :]
    sum_own[:, edge : edge + width] = nn(ones, dyv[...])[0:8, :]

    def sum_copy(step, g):
        if g:
            return remote(
                sum_own, sum_f.at[f], ss.at[0, g - 1], sr.at[0, g - 1], mate_to(g)
            )
        return remote(
            sum_own, sum_c.at[c], ss.at[1, step - 1], sr.at[1, step - 1], ctx_to(step)
        )

    sum_f[f] = sum_own[...]
    for g in range(1, nf):
        sum_copy(0, g).start()

    group = nc * own
    split = pieces_one + pieces_two

    def product(p, rows, second):
        lanes = pl.ds(pl.multiple_of(p * part, part), part)
        if second:
            return nn(dy_t[rows, :], oa[:, lanes])
        return nn(n_t[rows, :], gd[:, lanes])

    def half_copy(p, g):
        return remote(
            half_send.at[g - 1, p], half_recv.at[g - 1, p], hs.at[g - 1, p], hr.at[g - 1, p], mate_to(g)
        )

    def piece_copy(p, step):
        rows = pl.ds(pl.multiple_of(lax.rem(c + step, nc) * own, own), own)
        return remote(
            half_recv.at[0, p, rows],
            piece_recv.at[step - 1, p],
            ps.at[step - 1, p],
            pr.at[step - 1, p],
            ctx_to(step),
        )

    def give_half(p, base, second):
        for g in range(1, nf):
            rows = pl.ds(pl.multiple_of(lax.rem(f + g, nf) * group, group), group)
            half_send[g - 1, p] = product(p - base, rows, second).astype(BF16)
            half_copy(p, g).start()

    def keep_half(p, base, second):
        rows = pl.ds(pl.multiple_of(f * group, group), group)
        kept = product(p - base, rows, second)
        for g in range(1, nf):
            half_copy(p, g).wait_recv()
            kept = kept + half_recv[g - 1, p].astype(F32)
        half_recv[0, p] = kept.astype(BF16)
        for step in range(1, nc):
            piece_copy(p, step).start()

    def loop(low, high, body):
        lax.fori_loop(low, high, lambda i, carry: (body(i), carry)[1], 0)

    loop(0, pieces_one, lambda p: give_half(p, 0, False))
    loop(pieces_one, split, lambda p: give_half(p, pieces_one, True))
    loop(slots, chunks, lambda i: line_add(0, i))
    loop(0, chunks // 2, lambda i: line_back(0, i))
    loop(0, pieces_one, lambda p: keep_half(p, 0, False))
    loop(pieces_one, split, lambda p: keep_half(p, pieces_one, True))

    for g in range(1, nf):
        sum_copy(0, g).wait_recv()
        sum_copy(0, g).wait_send()
    held = sum_f[0]
    for i in range(1, nf):
        held = held + sum_f[i]
    sum_own[...] = held
    sum_c[c] = held
    for step in range(1, nc):
        sum_copy(step, 0).start()

    loop(0, chunks // 2, lambda i: line_add(1, i))
    loop(chunks // 2, chunks, lambda i: line_back(0, i))
    loop(chunks // 2, chunks, lambda i: line_add(1, i))

    for step in range(1, nc):
        sum_copy(step, 0).wait_recv()
        sum_copy(step, 0).wait_send()
    held = sum_c[0]
    for i in range(1, nc):
        held = held + sum_c[i]
    sums_out[...] = held

    def settle(p):
        rows = pl.ds(pl.multiple_of(c * own, own), own)
        kept = half_recv[0, p, rows, :].astype(F32)
        for step in range(1, nc):
            piece_copy(p, step).wait_recv()
            kept = kept + piece_recv[step - 1, p].astype(F32)
        dw_acc[:, pl.ds(pl.multiple_of(p * part, part), part)] = kept

    loop(0, split, settle)
    dw_store = pltpu.make_async_copy(dw_acc, dw_out, os.at[0])
    dw_store.start()

    loads_w = wsh[:, 0:edge].astype(F32)
    moment = dw_acc[:, 0:edge] * loads_w
    against = loads_w * sums_out[0:1, 0:edge]
    four = [
        jnp.sum(moment[:, 0:first], axis=1, keepdims=True),
        jnp.sum(against[:, 0:first], axis=1, keepdims=True),
        jnp.sum(moment[:, first:edge], axis=1, keepdims=True),
        jnp.sum(against[:, first:edge], axis=1, keepdims=True),
    ]
    lane = lax.broadcasted_iota(jnp.int32, (own, 128), 1)
    packed = jnp.zeros((own, 128), F32)
    for i, column in enumerate(four):
        packed = jnp.where(lane == i, column, packed)
    norm_own[...] = packed
    norm_in[t] = packed

    def norm_copy(k):
        return remote(norm_own, norm_in.at[t], ns.at[k - 1], nr.at[k - 1], tp_to(k))

    for k in range(1, nt_axis):
        norm_copy(k).start()

    loop(0, chunks, lambda i: line_back(1, i))

    for k in range(1, nt_axis):
        norm_copy(k).wait_recv()
        norm_copy(k).wait_send()
    held = norm_in[0]
    for i in range(1, nt_axis):
        held = held + norm_in[i]
    norms_out[...] = held

    for which in range(2):
        loop(0, chunks, functools.partial(line_done, which))
    for p in range(4):
        gather_sent(p)
    for step in range(1, nc):
        small_copy(step, 0).wait_send()
        kv_copy(step).wait_send()
        back_kv_copy(step).wait_send()
    for step in range(nc):
        for g in range(1, nf):
            small_copy(step, g).wait_send()

    def sent(p):
        for g in range(1, nf):
            half_copy(p, g).wait_send()
        for step in range(1, nc):
            piece_copy(p, step).wait_send()

    loop(0, split, sent)
    dw_store.wait()


def run_layer(sizes, *operands):
    nf, nc, tp = sizes["nf"], sizes["nc"], sizes["tp"]
    own, cols, ff, width = sizes["own"], sizes["cols"], sizes["ff"], sizes["width"]
    length, slots, total = sizes["length"], sizes["slots"], sizes["total"]
    part, split = sizes["part"], sizes["pieces_one"] + sizes["pieces_two"]
    rows = slots * length
    prompt = nc * length
    stacked = cols // HD * length
    edge = 3 * cols + ff
    chunks = rows // CHUNK
    sums = edge + width
    anywhere = pl.BlockSpec(memory_space=pl.ANY)
    vmem = pl.BlockSpec(memory_space=pltpu.VMEM)
    smem = pl.BlockSpec(memory_space=pltpu.SMEM)
    dma = pltpu.SemaphoreType.DMA
    shapes = (
        jax.ShapeDtypeStruct((rows, width), BF16),
        jax.ShapeDtypeStruct((rows, width), BF16),
        jax.ShapeDtypeStruct((own, total), F32),
        jax.ShapeDtypeStruct((8, sums), F32),
        jax.ShapeDtypeStruct((own, 128), F32),
        jax.ShapeDtypeStruct((8, width), F32),
    )
    half = nf - 1
    tmp = (8, 128)
    scratch = [
        pltpu.VMEM((rows, width), BF16),
        pltpu.VMEM((rows, width), BF16),
        pltpu.VMEM((width, rows), BF16),
        pltpu.VMEM((width, rows), BF16),
        pltpu.VMEM((width, total), BF16),
        pltpu.VMEM((own, total), BF16),
        pltpu.VMEM(tmp if sizes["turned"] else (cols, own), BF16),
        pltpu.VMEM(tmp if sizes["turned"] else (ff, own), BF16),
        pltpu.VMEM((rows, 1), F32),
        pltpu.VMEM((rows, 1), F32),
        pltpu.VMEM((rows, 128), F32),
        pltpu.VMEM((rows, 128), F32),
        pltpu.VMEM((nf * nc, 8, own), F32),
        pltpu.VMEM((rows, cols), BF16),
        pltpu.VMEM((rows, 2 * cols), BF16),
        pltpu.VMEM((prompt, 2 * cols), BF16),
        pltpu.VMEM((cols, prompt), BF16),
        pltpu.VMEM((cols, prompt), BF16),
        pltpu.VMEM((cols, length), BF16),
        pltpu.VMEM((cols, length), BF16),
        pltpu.VMEM((stacked, cols), BF16),
        pltpu.VMEM((stacked, cols), BF16),
        pltpu.VMEM((cols, length), F32),
        pltpu.VMEM((cols, length), F32),
        pltpu.VMEM((length, stacked), BF16),
        pltpu.VMEM((length, stacked), BF16),
        pltpu.VMEM((rows, cols), BF16),
        pltpu.VMEM((rows, cols + ff), BF16),
        pltpu.VMEM((rows, edge), BF16),
        pltpu.VMEM((prompt, 2 * cols), F32),
        pltpu.VMEM((nc - 1, length, 2 * cols), BF16),
        pltpu.VMEM((nc - 1, length, 2 * cols), BF16),
    ]
    scratch += [pltpu.VMEM((rows, width), BF16)] * 6
    scratch += [
        pltpu.VMEM((half, split, nc * own, part), BF16),
        pltpu.VMEM((half, split, nc * own, part), BF16),
        pltpu.VMEM((nc - 1, split, own, part), BF16),
        pltpu.VMEM((own, total), F32),
        pltpu.VMEM((8, sums), F32),
        pltpu.VMEM((nf, 8, sums), F32),
        pltpu.VMEM((nc, 8, sums), F32),
        pltpu.VMEM((own, 128), F32),
        pltpu.VMEM((tp, own, 128), F32),
        dma((10,)),
        dma((2, nc, nf)),
        dma((4, nc - 1)),
        dma((4, nc - 1)),
        dma((4, nc, half)),
        dma((4, nc, half)),
        dma((4,)),
        dma((nc - 1,)),
        dma((nc - 1,)),
        dma((nc - 1,)),
        dma((nc - 1,)),
        dma((2, chunks)),
        dma((2, chunks)),
        dma((2, chunks)),
        dma((2, chunks)),
        dma((2, chunks)),
        dma((half, split)),
        dma((half, split)),
        dma((nc - 1, split)),
        dma((nc - 1, split)),
        dma((2, max(half, nc - 1))),
        dma((2, max(half, nc - 1))),
        dma((tp - 1,)),
        dma((tp - 1,)),
        dma((1,)),
    ]
    return pl.pallas_call(
        functools.partial(layer_kernel, sizes),
        out_shape=shapes,
        in_specs=[smem, vmem] + [anywhere] * 8 + [vmem] * 3,
        out_specs=(anywhere, anywhere, anywhere, vmem, vmem, vmem),
        scratch_shapes=scratch,
        compiler_params=pltpu.CompilerParams(
            collective_id=0, has_side_effects=True, vmem_limit_bytes=62 * 1024 * 1024
        ),
        name="layer",
    )(*operands)


def on_device(
    x_prompt,
    x_cont,
    cont_start,
    w_qkv,
    qkv_bias,
    w_dense,
    dense_bias,
    w_fc1,
    fc1_bias,
    w_fc2,
    fc2_bias,
    ln1_gain,
    ln1_bias,
    ln2_gain,
    ln2_bias,
    dy_prompt,
    dy_cont,
):
    length = x_prompt.shape[1]
    conts, cont_len, width = x_cont.shape[1:]
    own, _, cols = w_qkv.shape
    ff = w_fc1.shape[1]
    nf, nc, tp = (lax.axis_size(name) for name in ("fsdp", "ctx", "tp"))
    edge = 3 * cols + ff
    part = 256 if edge % 256 == 0 and (cols + ff) % 256 == 0 else 128
    sizes = {
        "nf": nf,
        "nc": nc,
        "tp": tp,
        "own": own,
        "cols": cols,
        "ff": ff,
        "width": width,
        "length": length,
        "slots": 1 + conts,
        "total": 4 * cols + 2 * ff,
        "part": part,
        "pieces_one": edge // part,
        "pieces_two": (cols + ff) // part,
        "turned": own % 128 != 0,
    }
    turned = [w_dense.T, w_fc2.T] if sizes["turned"] else [w_dense, w_fc2]
    lane = np.arange(128) % HD
    inverse = 10000.0 ** (-2.0 * (lane % (ROT // 2)) / ROT)
    freq = np.zeros((8, 128), np.float32)
    freq[0] = np.where(lane < ROT, inverse, 0.0)
    freq[1] = np.where(lane < ROT // 2, -1.0, 1.0)
    small = jnp.stack([dense_bias, fc2_bias, ln1_gain, ln1_bias, ln2_gain, ln2_bias])
    small = jnp.pad(small.astype(F32), ((0, 2), (0, 0)))
    y_sum, u_sum, dw, sums, norms, small_full = run_layer(
        sizes,
        cont_start,
        jnp.asarray(freq),
        x_prompt[0],
        x_cont.reshape(conts * cont_len, width),
        dy_prompt[0],
        dy_cont.reshape(conts * cont_len, width),
        w_qkv.transpose(1, 0, 2),
        turned[0],
        w_fc1,
        turned[1],
        small,
        qkv_bias,
        fc1_bias.reshape(1, ff),
    )
    shift = small_full[0:1] + small_full[1:2]

    def finish(x, dy, y_rows, u_rows):
        x = x.astype(F32)
        centered = x - jnp.mean(x, axis=-1, keepdims=True)
        scale = lax.rsqrt(jnp.mean(centered * centered, axis=-1, keepdims=True) + EPS)
        unit = centered * scale
        u = u_rows.astype(F32)
        u = u - jnp.mean(u, axis=-1, keepdims=True) - unit * jnp.mean(u * unit, -1, keepdims=True)
        return x + y_rows.astype(F32) + shift, dy.astype(F32) + scale * u

    y_prompt, dx_prompt = finish(x_prompt[0], dy_prompt[0], y_sum[:length], u_sum[:length])
    tokens = conts * cont_len
    y_cont, dx_cont = finish(
        x_cont.reshape(tokens, width), dy_cont.reshape(tokens, width), y_sum[length:], u_sum[length:]
    )
    shape = x_cont.shape
    first = 3 * cols
    bias_q, bias_u = sums[0, :first], sums[0, first:edge]
    gain_one, shift_one = ln1_gain.astype(F32)[:, None], ln1_bias.astype(F32)[:, None]
    gain_two, shift_two = ln2_gain.astype(F32)[:, None], ln2_bias.astype(F32)[:, None]
    d_qkv = (dw[:, :first] * gain_one + shift_one * bias_q).reshape(own, 3, cols)
    d_fc1 = dw[:, first:edge] * gain_two + shift_two * bias_u
    d_dense = dw[:, edge : edge + cols].T
    d_fc2 = dw[:, edge + cols :].T
    place = (lax.axis_index("fsdp") * nc + lax.axis_index("ctx")) * own
    d_shift = lax.dynamic_slice_in_dim(sums[0, edge:], place, own)
    four = norms[:, 0:4].T
    return (
        y_prompt[None],
        y_cont.reshape(shape),
        dx_prompt[None],
        dx_cont.reshape(shape),
        d_qkv,
        bias_q.reshape(3, cols),
        d_dense,
        d_shift,
        d_fc1,
        bias_u,
        d_fc2,
        d_shift,
        four[0],
        four[1],
        four[2],
        four[3],
    )


def solution(mesh):
    both = ("fsdp", "ctx")
    rows = P("fsdp", "ctx", None)
    conts = P("fsdp", "ctx", None, None)
    vector = P(both)
    return jax.shard_map(
        on_device,
        mesh=mesh,
        in_specs=(
            rows,
            conts,
            P("fsdp", "ctx"),
            P(both, None, "tp"),
            P(None, "tp"),
            P("tp", both),
            vector,
            P(both, "tp"),
            P("tp"),
            P("tp", both),
            vector,
            vector,
            vector,
            vector,
            vector,
            rows,
            conts,
        ),
        out_specs=(
            rows,
            conts,
            rows,
            conts,
            P(both, None, "tp"),
            P(None, "tp"),
            P("tp", both),
            vector,
            P(both, "tp"),
            P("tp"),
            P("tp", both),
            vector,
            vector,
            vector,
            vector,
            vector,
        ),
        check_vma=False,
    )
```

time: 1050 us -> 252 us (0.24); the launches traced: 1040 us -> 252 us
  waiting for transfers between devices: 609 us -> 0 us
  Pallas kernels: 0 us -> 218 us
  blocking collectives: 159 us -> 0 us
  matrix products: 150 us -> 0 us
  other arithmetic: 76 us -> 24.4 us
  local copies, waits for them, and re-layouts: 27.1 us -> 8.47 us
  between operations: 15.5 us -> 0.81 us
    psum x2 -> x0, waiting for transfers between devices: 455 us -> none  [the longest x1 371 us: on_device(): attn_total = lax.psum(attn_part, 'tp')]
    pallas_call x0 -> x1, Pallas kernels: none -> 218 us  [run_layer(): pl.pallas_call(functools.partial(layer_kernel, sizes), out_shape=shapes,...]
    reduce_scatter x6 -> x0, waiting for transfers between devices: 153 us -> none  [the longest x1 55.6 us: on_device(): lax.psum_scatter(grad_down, ('fsdp', 'ctx'), scatter_dimension=1, tiled=T...]
    dot_general x18 -> x0, matrix products: 150 us -> none  [the longest x1 22 us: on_device(): jnp.einsum('qhd,khd->hqk', grad_attended, all_values, preferred_element_t...]
    all_gather x9 -> x0, blocking collectives: 132 us -> none  [the longest x1 25.5 us: on_device(): lax.all_gather(w_dense, ('fsdp', 'ctx'), axis=1, tiled=True)]
    reduce_sum x7 -> x6, other arithmetic: 38.1 us -> 9.14 us  [the longest x2 4.38 us: finish(): jnp.mean(u, axis=-1, keepdims=True)]
    psum x1 -> x0, blocking collectives: 26.6 us -> none  [on_device(): lax.psum((grad_qkv_bias, grad_up_bias), ('fsdp', 'ctx'))]
    convert_element_type x9 -> x4, other arithmetic: 26.4 us -> 2.75 us  [the longest x1 0.78 us: on_device(): ln1_gain.astype(F32)[:, None]]
  transfers between devices with their start and end apart: 11 -> 0, of which waited for: 6 -> 0; matrix products, arithmetic and copies ran while one was open for 23% -> 0% of each run, Pallas kernels for 0% -> 0%
where the time goes in v2:
time: 252 us
  Pallas kernels  218 us (87%)
  other arithmetic  24.4 us (10%)
  local copies, waits for them, and re-layouts  8.47 us (3%)
    pallas_call x1, Pallas kernels, run_layer(): pl.pallas_call(functools.partial(layer_kernel, sizes), out_shape=shapes,...  218 us

profile of v2, /device:TPU:0, one launch (start us, length us, event | category | flops | bytes accessed | tf_op | source)
XLA Modules:
  0.0 251.7 jit_solution(4162392212643813829)
XLA Ops:
  0.7 0.8 convert_element_type.52
  1.4 0.7 convert_element_type.53
  2.1 0.7 convert_element_type.54
  2.8 0.7 convert_element_type.55
  3.4 1.2 convert_reduce_fusion.3
  4.6 1.3 fusion.16
  5.9 0.8 stack.27
  7.3 1.3 reshape.121.refs_12_
  8.6 1.7 convert_reduce_fusion.1
  10.9 218.1 %layer.1 = (bf16[1024,1024]{1,0:T(8,128)(2,1)}, bf16[1024,1024]{1,0:T(8,128)(2,1)}, f32[128,3072]{1,0:T(8,128)}, f32[8,2816]{1,0:T(8,128)}, f32[128,128]{1,0:T(8,128)}, /*index=5*/f32[8,1024]{1,0:T(8,128)}) custom-call(s32[1,3]{1,0:T(1,128)} %refs_0_.1, f32[8,128]{1,0:T(8,128)} %constant.41.clone.refs_1_, bf16[256,1024]{1,0:T(8,128)(2,1)} %bitcast.39, ...), custom_call_target="tpu_custom_call" | custom-call | tf_op jit(solution)/shard_map/layer/pallas_call | solution.py:777
  229.0 0.9 fusion.20
  229.9 0.8 slice_reduce_fusion.4
  230.7 1.6 convert_reduce_fusion.2
  232.3 0.6 reshape_squeeze.3
  232.9 2.8 %convert_reduce_fusion = (f32[768]{0:T(1024)S(1)}, f32[768]{0:T(1024)S(1)}) fusion(bf16[1024,1024]{1,0:T(8,128)(2,1)} %get-tuple-element.24, f32[768]{0:T(1024)S(1)} %rsqrt.21, f32[768]{0:T(1024)S(1)} %div.33, bf16[1,3,256,1024]{3,2,1,0:T(8,128)(2,1)S(1)} %copy-done.1), kind=kLoop, calls=%fused_computation.2 | loop fusion | flops 5503488 | bytes 3158016 | tf_op jit(solution)/shard_map/reduce_sum | solution.py:864
  235.7 0.8 slice_reduce_fusion
  236.5 0.9 slice_bitcast_fusion.1
  237.4 0.8 copy.39
  238.1 1.1 multiply_add_fusion.1
  239.2 2.1 slice_bitcast_fusion
  241.4 1.0 copy.40
  242.5 0.9 copy.38
  243.5 3.2 %fusion.15 = (f32[1,256,1024]{2,1,0:T(8,128)}, f32[1,256,1024]{2,1,0:T(8,128)}) fusion(f32[256]{0:T(256)S(1)} %get-tuple-element.77, f32[256]{0:T(256)S(1)} %get-tuple-element.78, f32[256]{0:T(256)S(1)} %add_rsqrt_fusion.1, f32[256]{0:T(256)S(1)} %broadcast_multiply_fusion.5, bf16[1024,1024]{1,0:T(8,128)(2,1)} %get-tuple-element.24, ...), kind=kLoop, calls=%fused_computation.28 | loop fusion | flops 3407872 | bytes 4202496 | tf_op jit(solution)/shard_map/broadcast_in_dim | solution.py:887
  246.7 4.5 %fusion.5 = (f32[768,1024]{1,0:T(8,128)}, f32[768,1024]{1,0:T(8,128)}) fusion(f32[768]{0:T(1024)S(1)} %get-tuple-element.79, f32[768]{0:T(1024)S(1)} %div.33, f32[768]{0:T(1024)S(1)} %get-tuple-element.80, f32[768]{0:T(1024)S(1)} %rsqrt.21, bf16[1024,1024]{1,0:T(8,128)(2,1)S(1)} %copy-done.3, bf16[1,3,256,1024]{3,2,1,0:T(8,128)(2,1)S(1)} %copy-done.4, ...), kind=kLoop, calls=%fused_computation.12 | loop fusion | flops 10223616 | bytes 12599296 | tf_op jit(solution)/shard_map/add | solution.py:865
  (30 shorter events, 1.9 us)
Async XLA Ops:
  0.6 9.6 %copy-start = (bf16[1,3,256,1024]{3,2,1,0:T(8,128)(2,1)S(1)}, bf16[1,3,256,1024]{3,2,1,0:T(8,128)(2,1)}, u32[]{:S(2)}) copy-start(bf16[1,3,256,1024]{3,2,1,0:T(8,128)(2,1)} %param.19) | copy-start | bytes 4718596
  10.9 222.0 %copy-start.1 = (bf16[1,3,256,1024]{3,2,1,0:T(8,128)(2,1)S(1)}, bf16[1,3,256,1024]{3,2,1,0:T(8,128)(2,1)}, u32[]{:S(2)}) copy-start(bf16[1,3,256,1024]{3,2,1,0:T(8,128)(2,1)} %param.19) | copy-start | bytes 4718596
  229.0 6.7 %copy-start.5 = (f32[128,128]{1,0:T(8,128)S(1)}, f32[128,128]{1,0:T(8,128)}, u32[]{:S(2)}) copy-start(f32[128,128]{1,0:T(8,128)} %get-tuple-element.27) | copy-start | bytes 196612
  229.9 11.5 %copy-start.6 = (f32[1,1024]{1,0:T(1,128)}, f32[1,1024]{1,0:T(1,128)S(1)}, u32[]{:S(2)}) copy-start(f32[1,1024]{1,0:T(1,128)S(1)} %get-tuple-element.74) | copy-start | bytes 12292
  230.7 20.6 %copy-start.7 = (f32[128]{0:T(128)}, f32[128]{0:T(128)S(1)}, u32[]{:S(2)}) copy-start(f32[128]{0:T(128)S(1)} %dynamic-slice_bitcast_fusion) | copy-start | bytes 1540
  235.7 7.8 %copy-start.2 = (bf16[1,256,1024]{2,1,0:T(8,128)(2,1)S(1)}, bf16[1,256,1024]{2,1,0:T(8,128)(2,1)}, u32[]{:S(2)}) copy-start(bf16[1,256,1024]{2,1,0:T(8,128)(2,1)} %param.18) | copy-start | bytes 1572868
  243.5 3.2 %copy-start.3 = (bf16[1024,1024]{1,0:T(8,128)(2,1)S(1)}, bf16[1024,1024]{1,0:T(8,128)(2,1)}, u32[]{:S(2)}) copy-start(bf16[1024,1024]{1,0:T(8,128)(2,1)} %get-tuple-element.24) | copy-start | bytes 6291460
  243.5 3.2 %copy-start.4 = (bf16[1,3,256,1024]{3,2,1,0:T(8,128)(2,1)S(1)}, bf16[1,3,256,1024]{3,2,1,0:T(8,128)(2,1)}, u32[]{:S(2)}) copy-start(bf16[1,3,256,1024]{3,2,1,0:T(8,128)(2,1)} %param.34) | copy-start | bytes 4718596

commit v3 on v2

--- a/solution.py
+++ b/solution.py
@@ -16,6 +16,8 @@
 BF16 = jnp.bfloat16
 MESH = pl.DeviceIdType.MESH
 CHUNK = 128
+BLOCK = 128
+LAG = 2
 ERF = (0.254829592, -0.284496736, 1.421413741, -1.453152027, 1.061405429)
 
 
@@ -55,18 +57,26 @@
     own, cols, ff, width = sizes["own"], sizes["cols"], sizes["ff"], sizes["width"]
     length, slots, total = sizes["length"], sizes["slots"], sizes["total"]
     part, pieces_one, pieces_two = sizes["part"], sizes["pieces_one"], sizes["pieces_two"]
-    (
-        starts, freq, x_prompt, x_cont, dy_prompt, dy_cont, w_q, w_d, w_u, w_o,
-        small, bias_q, bias_u,
-        y_out, u_out, dw_out, sums_out, norms_out, small_out,
-        xv, dyv, n_t, dy_t, wall, wsh, wd_tmp, wo_tmp, mean_s, scale_s, cos_s, sin_s,
-        smallg, qb, kvb, kvp, k_t, v_t, ko_t, vo_t, qm, gm, o_t, dq_t, p_own, ds_own,
-        ga, oa, gd, acc, kv_send, kv_recv,
-        yb, ya, yt, ub, ua, ut, half_send, half_recv, piece_recv, dw_acc,
-        sum_own, sum_f, sum_c, norm_own, norm_in,
-        in_sem, small_sem, ws, wr, fs, fr, ls, kvs, kvr, gks, gkr,
-        zs, za, zbs, zb, zo, hs, hr, ps, pr, ss, sr, ns, nr, os,
-    ) = refs
+    turned_in = sizes["turned"]
+    refs = list(refs)
+
+    def take(count):
+        taken = refs[:count]
+        del refs[:count]
+        return taken
+
+    starts, freq, x_prompt, x_cont, dy_prompt, dy_cont, w_q, w_d, w_u, w_o = take(10)
+    vectors = take(1 if turned_in else 6)
+    bias_q, bias_up = take(2)
+    tot_out, dw_out, sums_out, norms_out, small_out = take(5)
+    xv, dyv, n_t, wall, wsh, wd_tmp, wo_tmp = take(7)
+    stat_s, cos_s, sin_s, small, smallg, bias_u = take(6)
+    qb, kvb, kvp, k_t, v_t, ko_t, vo_t, qm, gm, o_t, dq_t, p_own, ds_own, p_all = take(14)
+    ga, oa, gd, acc, kv_recv = take(5)
+    part_sum, from_out, from_in, half_send, half_recv, piece_recv, dw_acc = take(7)
+    sum_own, sum_f, sum_c, norm_own, norm_in = take(5)
+    in_sem, small_sem, ws, wr, fs, fr, ls, kvs, kvr, gks, gkr = take(11)
+    zs, za, zbs, zb, zo, hs, hr, ps, pr, ss, sr, ns, nr, os = take(14)
     f, c, t = lax.axis_index("fsdp"), lax.axis_index("ctx"), lax.axis_index("tp")
     heads = cols // HD
     rows_all = slots * length
@@ -81,6 +91,11 @@
 
     def ctx_from(step):
         return lax.rem(c + nc - step, nc)
+
+    across_x = c + 1 - 2 * lax.rem(c, 2)
+    across_y = lax.rem(c + 2, nc)
+    corner = lax.rem(across_x + 2, nc)
+    peers = (c, across_x, across_y, corner)
 
     def mate_to(step):
         return (lax.rem(f + step, nf), c, t)
@@ -109,7 +124,6 @@
         (w_q.at[2], wsh.at[:, pl.ds(2 * cols, cols)]),
         (w_u, wsh.at[:, pl.ds(first, ff)]),
     ]
-    turned_in = sizes["turned"]
     if turned_in:
         loads += [(w_d, wsh.at[:, pl.ds(edge, cols)]), (w_o, wsh.at[:, pl.ds(edge + cols, ff)])]
     else:
@@ -133,52 +147,84 @@
         (edge + cols, ff),
     )
 
-    def gather_copy(p, step, g):
-        lanes = pl.ds(spans[p][0], spans[p][1])
-        if g == 0:
-            return remote(
-                wsh.at[:, lanes],
-                wall.at[own_rows, lanes],
-                ws.at[p, step - 1],
-                wr.at[p, step - 1],
-                ctx_to(step),
-            )
-        held = f * nc + ctx_from(step)
-        rows = pl.ds(pl.multiple_of(held * own, own), own)
-        src = wsh.at[:, lanes] if step == 0 else wall.at[rows, lanes]
+    half_own = own // 2
+
+    def block(owner, side, size):
+        base = owner * size
+        if side is None:
+            return pl.ds(pl.multiple_of(base, size), size)
+        return pl.ds(pl.multiple_of(base + side * (size // 2), size // 2), size // 2)
+
+    routes = ((0, 0, 1), (0, 1, 2), (0, 1, 1), (0, 0, 2), (1, 0, 2), (2, 1, 1))
+    lands = ((1, 0), (2, 1), (1, 1), (2, 0), (3, 0), (3, 1))
+
+    def ctx_copy(route, source, target, size, send_sem, recv_sem):
+        owner, side, to = routes[route]
+        rows = block(peers[owner], side, size)
+        src = source(owner, side, rows)
+        return remote(src, target(rows), send_sem, recv_sem, (f, peers[to], t))
+
+    def lanes_of(p):
+        return pl.ds(spans[p][0], spans[p][1])
+
+    def gather_copy(p, route):
+        def source(owner, side, rows):
+            if owner == 0:
+                return wsh.at[pl.ds(side * half_own, half_own), lanes_of(p)]
+            return wall.at[pl.ds(rows.start + f * nc * own, half_own), lanes_of(p)]
+
+        def target(rows):
+            return wall.at[pl.ds(rows.start + f * nc * own, half_own), lanes_of(p)]
+
+        return ctx_copy(route, source, target, own, ws.at[p, route], wr.at[p, route])
+
+    def mate_copy(p, peer, g):
+        rows = block(f * nc + peers[peer], None, own)
+        src = wsh.at[:, lanes_of(p)] if peer == 0 else wall.at[rows, lanes_of(p)]
         return remote(
-            src, wall.at[rows, lanes], fs.at[p, step, g - 1], fr.at[p, step, g - 1], mate_to(g)
+            src,
+            wall.at[rows, lanes_of(p)],
+            fs.at[p, peer, g - 1],
+            fr.at[p, peer, g - 1],
+            mate_to(g),
         )
 
     def gather_local(p):
-        lanes = pl.ds(spans[p][0], spans[p][1])
-        return pltpu.make_async_copy(wsh.at[:, lanes], wall.at[own_rows, lanes], ls.at[p])
+        return pltpu.make_async_copy(
+            wsh.at[:, lanes_of(p)], wall.at[own_rows, lanes_of(p)], ls.at[p]
+        )
 
     def gather_start(p):
-        for step in range(1, nc):
-            gather_copy(p, step, 0).start()
+        for route in range(4):
+            gather_copy(p, route).start()
         for g in range(1, nf):
-            gather_copy(p, 0, g).start()
+            mate_copy(p, 0, g).start()
         gather_local(p).start()
 
+    def gather_relay(p):
+        for arrived, route in ((0, 4), (1, 5)):
+            gather_copy(p, arrived).wait_recv()
+            gather_copy(p, route).start()
+
     def gather_pass(p):
-        for step in range(1, nc):
-            gather_copy(p, step, 0).wait_recv()
+        for peer, rest in ((1, (2,)), (2, (3,)), (3, (4, 5))):
+            for route in rest:
+                gather_copy(p, route).wait_recv()
             for g in range(1, nf):
-                gather_copy(p, step, g).start()
+                mate_copy(p, peer, g).start()
 
     def gather_finish(p):
         gather_local(p).wait()
-        for step in range(nc):
+        for peer in range(nc):
             for g in range(1, nf):
-                gather_copy(p, step, g).wait_recv()
+                mate_copy(p, peer, g).wait_recv()
 
     def gather_sent(p):
-        for step in range(1, nc):
-            gather_copy(p, step, 0).wait_send()
-        for step in range(nc):
+        for route in range(6):
+            gather_copy(p, route).wait_send()
+        for peer in range(nc):
             for g in range(1, nf):
-                gather_copy(p, step, g).wait_send()
+                mate_copy(p, peer, g).wait_send()
 
     def small_copy(step, g):
         if g == 0:
@@ -191,6 +237,13 @@
             src, smallg.at[held], small_sem.at[0, step, g], small_sem.at[1, step, g], mate_to(g)
         )
 
+    if turned_in:
+        small[...] = vectors[0][...]
+    else:
+        small[...] = jnp.zeros_like(small)
+        for i, vector in enumerate(vectors):
+            small[i : i + 1, :] = vector[...].astype(F32).reshape(1, own)
+    bias_u[...] = bias_up[...].astype(F32).reshape(1, ff)
     for step in range(1, nc):
         small_copy(step, 0).start()
     for g in range(1, nf):
@@ -209,43 +262,45 @@
     loads[0].wait()
     loads[1].wait()
 
-    def statistics(slot, carry):
+    def statistics(slot):
         rows = pl.ds(pl.multiple_of(slot * length, length), length)
-        block = xv[rows, :].astype(F32)
-        mean = jnp.mean(block, axis=1, keepdims=True)
-        block = block - mean
-        scale = lax.rsqrt(jnp.mean(block * block, axis=1, keepdims=True) + EPS)
-        mean_s[rows, :] = mean
-        scale_s[rows, :] = scale
-        n_t[:, rows] = (block * scale).T.astype(BF16)
+        block_x = xv[rows, :].astype(F32)
+        mean = jnp.mean(block_x, axis=1, keepdims=True)
+        block_x = block_x - mean
+        scale = lax.rsqrt(jnp.mean(block_x * block_x, axis=1, keepdims=True) + EPS)
+        stat_s[rows, 0:1] = mean
+        stat_s[rows, 1:2] = scale
+        n_t[:, rows] = (block_x * scale).T.astype(BF16)
         before = starts[0, jnp.maximum(slot - 1, 0)]
         base = jnp.where(slot == 0, c * length, before)
         place = base + lax.broadcasted_iota(jnp.int32, (length, 128), 0)
         phase = place.astype(F32) * freq[0:1, :]
         cos_s[rows, :] = jnp.cos(phase)
         sin_s[rows, :] = jnp.sin(phase) * freq[1:2, :]
-        return carry
-
-    lax.fori_loop(0, slots, statistics, 0)
-
+
+    def loop(low, high, body):
+        lax.fori_loop(low, high, lambda i, carry: (body(i), carry)[1], 0)
+
+    statistics(0)
+    gather_relay(0)
     for step in range(1, nc):
         small_copy(step, 0).wait_recv()
         for g in range(1, nf):
             small_copy(step, g).start()
+    gather_relay(1)
+    gather_pass(0)
     for step in range(nc):
         for g in range(1, nf):
             small_copy(step, g).wait_recv()
     parts = [smallg[i] for i in range(nf * nc)]
-    whole = jnp.concatenate(parts, axis=1)
-    small_out[...] = whole
+    small_out[...] = jnp.concatenate(parts, axis=1)
     gain_one, shift_one = small_out[2:3, :], small_out[3:4, :]
     gain_two, shift_two = small_out[4:5, :], small_out[5:6, :]
 
     def normed(rows, gain, shift):
-        block = (xv[rows, :].astype(F32) - mean_s[rows, :]) * scale_s[rows, :]
+        block = (xv[rows, :].astype(F32) - stat_s[rows, 0:1]) * stat_s[rows, 1:2]
         return (block * gain + shift).astype(BF16)
 
-    gather_pass(0)
     gather_finish(0)
 
     def project(slot):
@@ -263,42 +318,49 @@
     mine = pl.ds(pl.multiple_of(c * length, length), length)
     kvp[mine, :] = kvb[0:length, :]
 
-    def kv_copy(step):
-        return remote(
-            kvb.at[pl.ds(0, length)], kvp.at[mine], kvs.at[step - 1], kvr.at[step - 1], ctx_to(step)
+    def kv_copy(route):
+        def source(owner, side, rows):
+            if owner == 0:
+                return kvb.at[pl.ds(side * (length // 2), length // 2)]
+            return kvp.at[rows]
+
+        return ctx_copy(
+            route, source, lambda rows: kvp.at[rows], length, kvs.at[route], kvr.at[route]
         )
 
-    for step in range(1, nc):
-        kv_copy(step).start()
+    for route in range(4):
+        kv_copy(route).start()
+    gather_pass(1)
     loads[7].wait()
-    gather_start(2)
     loads[9].wait()
     if not turned_in:
         wsh[:, edge + cols : total] = wo_tmp[...].astype(F32).T.astype(BF16)
+    loop(1, slots // 2 + 1, statistics)
+    for arrived, route in ((0, 4), (1, 5)):
+        kv_copy(arrived).wait_recv()
+        kv_copy(route).start()
+    gather_start(2)
     gather_start(3)
-
-    lax.fori_loop(1, slots, lambda slot, carry: (project(slot), carry)[1], 0)
-
-    gather_pass(1)
+    loop(slots // 2 + 1, slots, statistics)
+    loop(1, slots, project)
     gather_finish(1)
     loads[2].wait()
     loads[3].wait()
-
-    def back_dense(slot, carry):
+    gather_relay(2)
+
+    def back_dense(slot):
         rows = pl.ds(pl.multiple_of(slot * length, length), length)
-        block = dyv[rows, :]
-        ga[rows, :] = nn(block, wall[:, edge : edge + cols]).astype(BF16)
-        dy_t[:, rows] = block.astype(F32).T.astype(BF16)
-        return carry
-
-    lax.fori_loop(0, slots, back_dense, 0)
-
-    for step in range(1, nc):
-        kv_copy(step).wait_recv()
+        block_dy = dyv[rows, :]
+        ga[rows, :] = nn(block_dy, wall[:, edge : edge + cols]).astype(BF16)
+
+    loop(0, slots, back_dense)
+
+    for route in range(2, 6):
+        kv_copy(route).wait_recv()
     k_t[...] = kvp[:, 0:cols].astype(F32).T.astype(BF16)
     v_t[...] = kvp[:, cols : 2 * cols].astype(F32).T.astype(BF16)
 
-    def attend(slot, is_prompt):
+    def attend(slot, is_prompt, between=()):
         rows = pl.ds(pl.multiple_of(slot * length, length), length)
         head_of = lax.div(lax.broadcasted_iota(jnp.int32, (length, cols), 1), HD)
         query, grad = qb[rows, :], ga[rows, :]
@@ -338,7 +400,7 @@
             share = 1.0 / norm
             probs = probs * share
             probs_low = probs.astype(BF16)
-            yb[0:prompt, lanes] = probs_low
+            p_all[0, 0:prompt, lanes] = probs_low
             grads = nt(kvp[:, cols : 2 * cols], g_h)
             inner = jnp.sum(probs * grads, axis=0, keepdims=True)
             if not is_prompt:
@@ -348,7 +410,7 @@
                 grads_own = nt(kvb[rows, cols : 2 * cols], g_h)
                 inner = inner + jnp.sum(probs_own * grads_own, axis=0, keepdims=True)
             back_low = (probs * (grads - inner)).astype(BF16)
-            ub[0:prompt, lanes] = back_low
+            p_all[1, 0:prompt, lanes] = back_low
             out_t = nn(v_t[lines, :], probs_low)
             back_q = nn(k_t[lines, :], back_low)
             if not is_prompt:
@@ -358,6 +420,8 @@
                 back_q = back_q + nn(ko_t[lines, :], back_own)
             o_t[lines, :] = out_t
             dq_t[lines, :] = back_q
+            for at, action in between:
+                pl.when(h == at)(action)
             return carry
 
         lax.fori_loop(0, heads, one_head, 0)
@@ -365,123 +429,129 @@
         oa[rows, 0:cols] = o_t[...].T.astype(BF16)
         gd[rows, 0:cols] = turn(dq_t[...].T * 0.125, cos_t, sin_t).astype(BF16)
         stacked = heads * length
-        back_k = nn(ub[0:prompt, 0:stacked], qm[...])
-        back_v = nn(yb[0:prompt, 0:stacked], gm[...])
-        if is_prompt:
-            acc[:, 0:cols] = back_k
-            acc[:, cols : 2 * cols] = back_v
-        else:
-            acc[:, 0:cols] += back_k
-            acc[:, cols : 2 * cols] += back_v
+        back_k = nn(p_all[1, 0:prompt, 0:stacked], qm[...])
+        back_v = nn(p_all[0, 0:prompt, 0:stacked], gm[...])
+        acc[:, 0:cols] += back_k
+        acc[:, cols : 2 * cols] += back_v
+        if not is_prompt:
             gd[rows, cols : 2 * cols] = turn(nn(ds_own[...], qm[...]), cos_t, sin_t).astype(BF16)
             gd[rows, 2 * cols : first] = nn(p_own[...], gm[...]).astype(BF16)
 
-    attend(0, True)
-    lax.fori_loop(1, slots, lambda slot, carry: (attend(slot, False), carry)[1], 0)
+    def kv_send(step):
+        return p_all.at[1, pl.ds((step - 1) * length, length), pl.ds(0, 2 * cols)]
 
     def back_kv_copy(step):
         return remote(
-            kv_send.at[step - 1], kv_recv.at[step - 1], gks.at[step - 1], gkr.at[step - 1], ctx_to(step)
+            kv_send(step), kv_recv.at[step - 1], gks.at[step - 1], gkr.at[step - 1], ctx_to(step)
         )
 
-    for step in range(1, nc):
-        there = pl.ds(pl.multiple_of(lax.rem(c + step, nc) * length, length), length)
-        kv_send[step - 1] = acc[there, :].astype(BF16)
-        back_kv_copy(step).start()
-
     chunks = rows_all // CHUNK
-    sums = ((yb, ya, yt, y_out), (ub, ua, ut, u_out))
-
-    def line(which, i):
-        return sums[which], pl.ds(pl.multiple_of(i * CHUNK, CHUNK), CHUNK)
-
-    def line_out(which, i, middle):
-        (mine_ref, from_out, from_in, _), rows = line(which, i)
+    per_slot = length // CHUNK
+    pair = slots // 2
+
+    def line(q):
+        group, inner = lax.div(q, per_slot), lax.rem(q, per_slot)
+        which = lax.rem(lax.div(group, pair), 2)
+        slot = lax.rem(lax.div(group, 2 * pair) * pair + lax.rem(group, pair) + 1, slots)
+        return which, pl.ds(pl.multiple_of((slot * per_slot + inner) * CHUNK, CHUNK), CHUNK)
+
+    def line_out(q, middle):
+        which, rows = line(q)
         target = from_in if middle else from_out
         landed = zb if middle else za
         return remote(
-            mine_ref.at[rows], target.at[rows], zs.at[which, i], landed.at[which, i], inward
+            part_sum.at[which, rows], target.at[which, rows], zs.at[q], landed.at[q], inward
         )
 
-    def line_home(which, i, middle):
-        (_, from_out, from_in, _), rows = line(which, i)
+    def line_home(q, middle):
+        which, rows = line(q)
         src = from_out if middle else from_in
         return remote(
-            src.at[rows], from_in.at[rows], zbs.at[which, i], zb.at[which, i], outward
+            src.at[which, rows], from_in.at[which, rows], zbs.at[q], zb.at[q], outward
         )
 
-    def line_store(which, i, middle):
-        (_, from_out, from_in, out), rows = line(which, i)
+    def line_store(q, middle):
+        which, rows = line(q)
         src = from_out if middle else from_in
-        return pltpu.make_async_copy(src.at[rows], out.at[rows], zo.at[which, i])
-
-    def line_send(which, i):
+        return pltpu.make_async_copy(src.at[which, rows], tot_out.at[which, rows], zo.at[q])
+
+    def line_send(q):
         @pl.when(in_middle)
         def _():
-            line_out(which, i, True).start()
+            line_out(q, True).start()
 
         @pl.when(not_middle)
         def _():
-            line_out(which, i, False).start()
-
-    def line_first(which, i):
+            line_out(q, False).start()
+
+    def line_first(q):
         @pl.when(at_end)
         def _():
-            line_send(which, i)
-
-    def line_add(which, i):
-        (mine_ref, from_out, _, _), rows = line(which, i)
+            line_send(q)
+
+    def line_add(q):
+        which, rows = line(q)
 
         @pl.when(not_end)
         def _():
-            line_out(which, i, False).wait_recv()
-            mine_ref[rows, :] = (
-                mine_ref[rows, :].astype(F32) + from_out[rows, :].astype(F32)
+            line_out(q, False).wait_recv()
+            part_sum[which, rows, :] = (
+                part_sum[which, rows, :].astype(F32) + from_out[which, rows, :].astype(F32)
             ).astype(BF16)
-            line_send(which, i)
-
-    def line_back(which, i):
-        (mine_ref, from_out, from_in, _), rows = line(which, i)
+            line_send(q)
+
+    def line_back(q):
+        which, rows = line(q)
 
         @pl.when(in_middle)
         def _():
-            line_out(which, i, True).wait_recv()
-            from_out[rows, :] = (
-                mine_ref[rows, :].astype(F32) + from_in[rows, :].astype(F32)
+            line_out(q, True).wait_recv()
+            from_out[which, rows, :] = (
+                part_sum[which, rows, :].astype(F32) + from_in[which, rows, :].astype(F32)
             ).astype(BF16)
 
             @pl.when(not_end)
             def _():
-                line_home(which, i, True).start()
-
-            line_store(which, i, True).start()
+                line_home(q, True).start()
+
+            line_store(q, True).start()
 
         @pl.when(not_middle)
         def _():
-            line_home(which, i, False).wait_recv()
+            line_home(q, False).wait_recv()
 
             @pl.when(not_end)
             def _():
-                line_home(which, i, False).start()
-
-            line_store(which, i, False).start()
-
-    def line_done(which, i):
-        line_out(which, i, True).wait_send()
-        line_store(which, i, True).wait()
+                line_home(q, False).start()
+
+            line_store(q, False).start()
+
+    def line_done(q):
+        line_out(q, True).wait_send()
+        line_store(q, True).wait()
 
         @pl.when(not_end)
         def _():
-            line_home(which, i, True).wait_send()
-
-    for p in (2, 3):
-        gather_pass(p)
-    for p in (2, 3):
-        gather_finish(p)
-
-    def feed(slot, carry):
-        rows = pl.ds(pl.multiple_of(slot * length, length), length)
-        hidden = nn(normed(rows, gain_two, shift_two), wall[:, first:edge]) + bias_u[...].astype(F32)
+            line_home(q, True).wait_send()
+
+    def tick(q):
+        @pl.when(q < 2 * chunks)
+        def _():
+            line_add(q)
+
+        @pl.when((q >= LAG) & not_end)
+        def _():
+            line_back(q - LAG)
+
+    def first_chunks(position, which):
+        half_at, inner = divmod(position, pair)
+        group = half_at * 2 * pair + which * pair + inner
+        return group * per_slot
+
+    def feed(position):
+        slot = (position + 1) % slots
+        rows = pl.ds(slot * length, length)
+        hidden = nn(normed(rows, gain_two, shift_two), wall[:, first:edge]) + bias_u[...]
         depth = jnp.abs(hidden) * np.float32(0.5**0.5)
         step = 1.0 / (1.0 + np.float32(0.3275911) * depth)
         poly = np.float32(ERF[4])
@@ -494,13 +564,52 @@
         slope = below + hidden * (bell * np.float32((2.0 * np.pi) ** -0.5))
         back = nn(dyv[rows, :], wall[:, edge + cols : total])
         gd[rows, first:edge] = (back * slope).astype(BF16)
-        yb[rows, :] = nt(oa[rows, :], wall[:, edge:total]).astype(BF16)
-        for i in range(length // CHUNK):
-            line_first(0, slot * (length // CHUNK) + i)
-        return carry
-
-    lax.fori_loop(0, slots, feed, 0)
-
+        part_sum[0, rows, :] = nt(oa[rows, :], wall[:, edge:total]).astype(BF16)
+        for i in range(per_slot):
+            line_first(first_chunks(position, 0) + i)
+
+    def back_norms(position):
+        slot = (position + 1) % slots
+        rows = pl.ds(slot * length, length)
+        toward_x = nt(gd[rows, 0:first], wall[:, 0:first]) * gain_one
+        toward_x = toward_x + nt(gd[rows, first:edge], wall[:, first:edge]) * gain_two
+        part_sum[1, rows, :] = toward_x.astype(BF16)
+        for i in range(per_slot):
+            line_first(first_chunks(position, 1) + i)
+
+    acc[...] = jnp.zeros_like(acc)
+    loop(1, pair + 1, lambda slot: attend(slot, False))
+    gather_relay(3)
+    for p in (2, 3):
+        gather_pass(p)
+    for p in (2, 3):
+        gather_finish(p)
+    for position in range(pair):
+        feed(position)
+    for position in range(pair):
+        back_norms(position)
+    for slot in range(pair + 1, slots):
+        attend(slot, False, ((heads - 1, lambda: tick(0)),))
+    attend(0, True, ((0, lambda: tick(1)), (heads - 1, lambda: tick(2))))
+
+    for step in range(1, nc):
+        there = pl.ds(pl.multiple_of(lax.rem(c + step, nc) * length, length), length)
+        kv_send(step)[...] = acc[there, :].astype(BF16)
+        back_kv_copy(step).start()
+
+    for position in range(pair, slots):
+        feed(position)
+    tick(3)
+
+    def turn_dy(slot):
+        rows = pl.ds(pl.multiple_of(slot * length, length), length)
+        p_all[0, :, rows] = dyv[rows, :].astype(F32).T.astype(BF16)
+
+    loop(0, slots, turn_dy)
+    for position in range(pair, slots - 1):
+        back_norms(position)
+
+    tick(4)
     grad_kv = acc[mine, :]
     for step in range(1, nc):
         back_kv_copy(step).wait_recv()
@@ -509,18 +618,7 @@
         grad_kv[:, 0:cols], cos_s[0:length, :], -sin_s[0:length, :]
     ).astype(BF16)
     gd[0:length, 2 * cols : first] = grad_kv[:, cols : 2 * cols].astype(BF16)
-
-    def back_norms(slot, carry):
-        rows = pl.ds(pl.multiple_of(slot * length, length), length)
-        toward_x = nt(gd[rows, 0:first], wall[:, 0:first]) * gain_one
-        toward_x = toward_x + nt(gd[rows, first:edge], wall[:, first:edge]) * gain_two
-        ub[rows, :] = toward_x.astype(BF16)
-        for i in range(length // CHUNK):
-            line_first(1, slot * (length // CHUNK) + i)
-        line_add(0, slot)
-        return carry
-
-    lax.fori_loop(0, slots, back_norms, 0)
+    back_norms(slots - 1)
 
     ones = jnp.ones((16, rows_all), BF16)
     sum_own[:, 0:edge] = nn(ones, gd[...])[0:8, :]
@@ -545,7 +643,7 @@
     def product(p, rows, second):
         lanes = pl.ds(pl.multiple_of(p * part, part), part)
         if second:
-            return nn(dy_t[rows, :], oa[:, lanes])
+            return nn(p_all[0, rows, :], oa[:, lanes])
         return nn(n_t[rows, :], gd[:, lanes])
 
     def half_copy(p, g):
@@ -579,15 +677,20 @@
         for step in range(1, nc):
             piece_copy(p, step).start()
 
-    def loop(low, high, body):
-        lax.fori_loop(low, high, lambda i, carry: (body(i), carry)[1], 0)
-
     loop(0, pieces_one, lambda p: give_half(p, 0, False))
     loop(pieces_one, split, lambda p: give_half(p, pieces_one, True))
-    loop(slots, chunks, lambda i: line_add(0, i))
-    loop(0, chunks // 2, lambda i: line_back(0, i))
-    loop(0, pieces_one, lambda p: keep_half(p, 0, False))
-    loop(pieces_one, split, lambda p: keep_half(p, pieces_one, True))
+    tick(5)
+
+    def keep_and_tick(p, base, second):
+        keep_half(p, base, second)
+
+        @pl.when(lax.rem(p, 2) == 1)
+        def _():
+            tick(6 + lax.div(p, 2))
+
+    loop(0, pieces_one, lambda p: keep_and_tick(p, 0, False))
+    loop(pieces_one, split, lambda p: keep_and_tick(p, pieces_one, True))
+    ticked = 6 + split // 2
 
     for g in range(1, nf):
         sum_copy(0, g).wait_recv()
@@ -600,9 +703,7 @@
     for step in range(1, nc):
         sum_copy(step, 0).start()
 
-    loop(0, chunks // 2, lambda i: line_add(1, i))
-    loop(chunks // 2, chunks, lambda i: line_back(0, i))
-    loop(chunks // 2, chunks, lambda i: line_add(1, i))
+    loop(ticked, ticked + 2, tick)
 
     for step in range(1, nc):
         sum_copy(step, 0).wait_recv()
@@ -646,7 +747,18 @@
     for k in range(1, nt_axis):
         norm_copy(k).start()
 
-    loop(0, chunks, lambda i: line_back(1, i))
+    def finish_line(q):
+        tick(q)
+
+        @pl.when(at_end)
+        def _():
+            line_back(q - LAG)
+
+    @pl.when(at_end)
+    def _():
+        loop(0, ticked + 2 - LAG, line_back)
+
+    loop(ticked + 2, 2 * chunks + LAG, finish_line)
 
     for k in range(1, nt_axis):
         norm_copy(k).wait_recv()
@@ -656,14 +768,14 @@
         held = held + norm_in[i]
     norms_out[...] = held
 
-    for which in range(2):
-        loop(0, chunks, functools.partial(line_done, which))
+    loop(0, 2 * chunks, line_done)
     for p in range(4):
         gather_sent(p)
     for step in range(1, nc):
         small_copy(step, 0).wait_send()
-        kv_copy(step).wait_send()
         back_kv_copy(step).wait_send()
+    for route in range(6):
+        kv_copy(route).wait_send()
     for step in range(nc):
         for g in range(1, nf):
             small_copy(step, g).wait_send()
@@ -694,8 +806,7 @@
     smem = pl.BlockSpec(memory_space=pltpu.SMEM)
     dma = pltpu.SemaphoreType.DMA
     shapes = (
-        jax.ShapeDtypeStruct((rows, width), BF16),
-        jax.ShapeDtypeStruct((rows, width), BF16),
+        jax.ShapeDtypeStruct((2, rows, width), BF16),
         jax.ShapeDtypeStruct((own, total), F32),
         jax.ShapeDtypeStruct((8, sums), F32),
         jax.ShapeDtypeStruct((own, 128), F32),
@@ -707,16 +818,16 @@
         pltpu.VMEM((rows, width), BF16),
         pltpu.VMEM((rows, width), BF16),
         pltpu.VMEM((width, rows), BF16),
-        pltpu.VMEM((width, rows), BF16),
         pltpu.VMEM((width, total), BF16),
         pltpu.VMEM((own, total), BF16),
         pltpu.VMEM(tmp if sizes["turned"] else (cols, own), BF16),
         pltpu.VMEM(tmp if sizes["turned"] else (ff, own), BF16),
-        pltpu.VMEM((rows, 1), F32),
-        pltpu.VMEM((rows, 1), F32),
+        pltpu.VMEM((rows, 2), F32),
         pltpu.VMEM((rows, 128), F32),
         pltpu.VMEM((rows, 128), F32),
+        pltpu.VMEM((8, own), F32),
         pltpu.VMEM((nf * nc, 8, own), F32),
+        pltpu.VMEM((1, ff), F32),
         pltpu.VMEM((rows, cols), BF16),
         pltpu.VMEM((rows, 2 * cols), BF16),
         pltpu.VMEM((prompt, 2 * cols), BF16),
@@ -730,14 +841,14 @@
         pltpu.VMEM((cols, length), F32),
         pltpu.VMEM((length, stacked), BF16),
         pltpu.VMEM((length, stacked), BF16),
+        pltpu.VMEM((2, max(prompt, width), max(stacked, rows)), BF16),
         pltpu.VMEM((rows, cols), BF16),
         pltpu.VMEM((rows, cols + ff), BF16),
         pltpu.VMEM((rows, edge), BF16),
         pltpu.VMEM((prompt, 2 * cols), F32),
         pltpu.VMEM((nc - 1, length, 2 * cols), BF16),
-        pltpu.VMEM((nc - 1, length, 2 * cols), BF16),
     ]
-    scratch += [pltpu.VMEM((rows, width), BF16)] * 6
+    scratch += [pltpu.VMEM((2, rows, width), BF16)] * 3
     scratch += [
         pltpu.VMEM((half, split, nc * own, part), BF16),
         pltpu.VMEM((half, split, nc * own, part), BF16),
@@ -750,20 +861,20 @@
         pltpu.VMEM((tp, own, 128), F32),
         dma((10,)),
         dma((2, nc, nf)),
-        dma((4, nc - 1)),
-        dma((4, nc - 1)),
+        dma((4, 6)),
+        dma((4, 6)),
         dma((4, nc, half)),
         dma((4, nc, half)),
         dma((4,)),
+        dma((6,)),
+        dma((6,)),
         dma((nc - 1,)),
         dma((nc - 1,)),
-        dma((nc - 1,)),
-        dma((nc - 1,)),
-        dma((2, chunks)),
-        dma((2, chunks)),
-        dma((2, chunks)),
-        dma((2, chunks)),
-        dma((2, chunks)),
+        dma((2 * chunks,)),
+        dma((2 * chunks,)),
+        dma((2 * chunks,)),
+        dma((2 * chunks,)),
+        dma((2 * chunks,)),
         dma((half, split)),
         dma((half, split)),
         dma((nc - 1, split)),
@@ -777,13 +888,114 @@
     return pl.pallas_call(
         functools.partial(layer_kernel, sizes),
         out_shape=shapes,
-        in_specs=[smem, vmem] + [anywhere] * 8 + [vmem] * 3,
-        out_specs=(anywhere, anywhere, anywhere, vmem, vmem, vmem),
+        in_specs=[smem, vmem] + [anywhere] * 8 + [vmem] * (len(operands) - 10),
+        out_specs=(anywhere, anywhere, vmem, vmem, vmem),
         scratch_shapes=scratch,
         compiler_params=pltpu.CompilerParams(
-            collective_id=0, has_side_effects=True, vmem_limit_bytes=62 * 1024 * 1024
+            collective_id=0, has_side_effects=True, vmem_limit_bytes=63 * 1024 * 1024
         ),
         name="layer",
+    )(*operands)
+
+
+def close_kernel(sizes, *refs):
+    nc, own, cols, ff = sizes["nc"], sizes["own"], sizes["cols"], sizes["ff"]
+    first, turned = 3 * cols, sizes["turned"]
+    edge = first + ff
+    prompt_blocks = sizes["length"] // BLOCK
+    refs = list(refs)
+
+    def take(count):
+        taken = refs[:count]
+        del refs[:count]
+        return taken
+
+    x_prompt, x_cont, dy_prompt, dy_cont, totals, shifts, dw, sums, norms = take(9)
+    gains = take(1 if turned else 4)
+    y_prompt, y_cont, dx_prompt, dx_cont, d_qkv, b_qkv, d_dense, d_u, b_u, d_o = take(10)
+    rest = take(1 if turned else 2)
+    at = pl.program_id(0)
+
+    def rows_of(x_ref, dy_ref, y_ref, dx_ref):
+        x = x_ref[...].astype(F32)
+        u = totals[1].astype(F32)
+        centered = x - jnp.mean(x, axis=1, keepdims=True)
+        scale = lax.rsqrt(jnp.mean(centered * centered, axis=1, keepdims=True) + EPS)
+        unit = centered * scale
+        u = u - jnp.mean(u, axis=1, keepdims=True) - unit * jnp.mean(u * unit, axis=1, keepdims=True)
+        y_ref[...] = x + totals[0].astype(F32) + (shifts[0:1, :] + shifts[1:2, :])
+        dx_ref[...] = dy_ref[...].astype(F32) + scale * u
+
+    @pl.when(at < prompt_blocks)
+    def _():
+        rows_of(x_prompt, dy_prompt, y_prompt, dx_prompt)
+
+    @pl.when(at >= prompt_blocks)
+    def _():
+        rows_of(x_cont, dy_cont, y_cont, dx_cont)
+
+    @pl.when(at == 0)
+    def _():
+        if turned:
+            gain_one, shift_one, gain_two, shift_two = (gains[0][:, i : i + 1] for i in range(4))
+        else:
+            rows = [ref[...].astype(F32).reshape(1, own) for ref in gains]
+            columns = jnp.concatenate(rows * 2, axis=0).T
+            gain_one, shift_one, gain_two, shift_two = (columns[:, i : i + 1] for i in range(4))
+        for i in range(3):
+            lanes = slice(i * cols, (i + 1) * cols)
+            total = sums[0:1, lanes]
+            d_qkv[i] = dw[:, lanes] * gain_one + shift_one * total
+            b_qkv[i : i + 1, :] = total
+        total = sums[0:1, first:edge]
+        d_u[...] = dw[:, first:edge] * gain_two + shift_two * total
+        b_u[...] = total
+        if turned:
+            d_dense[...] = dw[:, edge : edge + cols]
+            d_o[...] = dw[:, edge + cols :]
+            rest[0][...] = norms[...]
+        else:
+            d_dense[...] = dw[:, edge : edge + cols].T
+            d_o[...] = dw[:, edge + cols :].T
+            rest[0][...] = norms[...].T[0:8, :]
+            shard = lax.axis_index("fsdp") * nc + lax.axis_index("ctx")
+            lanes = pl.ds(pl.multiple_of(edge + shard * own, own), own)
+            rest[1][...] = sums[0:1, lanes]
+
+
+def close_layer(sizes, *operands):
+    own, cols, ff, width = sizes["own"], sizes["cols"], sizes["ff"], sizes["width"]
+    length, slots, turned = sizes["length"], sizes["slots"], sizes["turned"]
+    near = length // BLOCK
+    blocks = slots * near
+    prompt = pl.BlockSpec((BLOCK, width), lambda i: (jnp.minimum(i, near - 1), 0))
+    cont = pl.BlockSpec((BLOCK, width), lambda i: (jnp.maximum(i - near, 0), 0))
+    both = pl.BlockSpec((2, BLOCK, width), lambda i: (0, i, 0))
+
+    def fixed(*shape):
+        return pl.BlockSpec(shape, lambda i: (0,) * len(shape))
+
+    def array(*shape):
+        return jax.ShapeDtypeStruct(shape, F32)
+
+    kept = [
+        (3, own, cols),
+        (3, cols),
+        (own, cols) if turned else (cols, own),
+        (own, ff),
+        (1, ff),
+        (own, ff) if turned else (ff, own),
+    ]
+    kept += [(own, 128)] if turned else [(8, own), (1, own)]
+    rows_prompt, rows_cont = array(length, width), array((slots - 1) * length, width)
+    return pl.pallas_call(
+        functools.partial(close_kernel, sizes),
+        grid=(blocks,),
+        in_specs=[prompt, cont, prompt, cont, both] + [fixed(*o.shape) for o in operands[5:]],
+        out_specs=[prompt, cont, prompt, cont] + [fixed(*shape) for shape in kept],
+        out_shape=[rows_prompt, rows_cont, rows_prompt, rows_cont] + [array(*s) for s in kept],
+        compiler_params=pltpu.CompilerParams(vmem_limit_bytes=62 * 1024 * 1024),
+        name="close",
     )(*operands)
 
 
@@ -835,9 +1047,10 @@
     freq = np.zeros((8, 128), np.float32)
     freq[0] = np.where(lane < ROT, inverse, 0.0)
     freq[1] = np.where(lane < ROT // 2, -1.0, 1.0)
-    small = jnp.stack([dense_bias, fc2_bias, ln1_gain, ln1_bias, ln2_gain, ln2_bias])
-    small = jnp.pad(small.astype(F32), ((0, 2), (0, 0)))
-    y_sum, u_sum, dw, sums, norms, small_full = run_layer(
+    vectors = [dense_bias, fc2_bias, ln1_gain, ln1_bias, ln2_gain, ln2_bias]
+    if sizes["turned"]:
+        vectors = [jnp.pad(jnp.stack(vectors).astype(F32), ((0, 2), (0, 0)))]
+    totals, dw, sums, norms, small_full = run_layer(
         sizes,
         cont_start,
         jnp.asarray(freq),
@@ -849,50 +1062,47 @@
         turned[0],
         w_fc1,
         turned[1],
-        small,
+        *vectors,
         qkv_bias,
-        fc1_bias.reshape(1, ff),
+        fc1_bias,
     )
-    shift = small_full[0:1] + small_full[1:2]
-
-    def finish(x, dy, y_rows, u_rows):
-        x = x.astype(F32)
-        centered = x - jnp.mean(x, axis=-1, keepdims=True)
-        scale = lax.rsqrt(jnp.mean(centered * centered, axis=-1, keepdims=True) + EPS)
-        unit = centered * scale
-        u = u_rows.astype(F32)
-        u = u - jnp.mean(u, axis=-1, keepdims=True) - unit * jnp.mean(u * unit, -1, keepdims=True)
-        return x + y_rows.astype(F32) + shift, dy.astype(F32) + scale * u
-
-    y_prompt, dx_prompt = finish(x_prompt[0], dy_prompt[0], y_sum[:length], u_sum[:length])
+    gains = [ln1_gain, ln1_bias, ln2_gain, ln2_bias]
+    if sizes["turned"]:
+        gains = [jnp.stack(gains, axis=1).astype(F32)]
     tokens = conts * cont_len
-    y_cont, dx_cont = finish(
-        x_cont.reshape(tokens, width), dy_cont.reshape(tokens, width), y_sum[length:], u_sum[length:]
+    closed = close_layer(
+        sizes,
+        x_prompt[0],
+        x_cont.reshape(tokens, width),
+        dy_prompt[0],
+        dy_cont.reshape(tokens, width),
+        totals,
+        small_full,
+        dw,
+        sums,
+        norms,
+        *gains,
     )
+    y_prompt, y_cont, dx_prompt, dx_cont, d_qkv, b_qkv, d_dense, d_u, b_u, d_o = closed[:10]
+    if sizes["turned"]:
+        d_dense, d_o, four = d_dense.T, d_o.T, closed[10][:, 0:4].T
+        place = (lax.axis_index("fsdp") * nc + lax.axis_index("ctx")) * own
+        d_shift = lax.dynamic_slice_in_dim(sums[0, edge:], place, own)
+    else:
+        four, d_shift = closed[10], closed[11].reshape(own)
     shape = x_cont.shape
-    first = 3 * cols
-    bias_q, bias_u = sums[0, :first], sums[0, first:edge]
-    gain_one, shift_one = ln1_gain.astype(F32)[:, None], ln1_bias.astype(F32)[:, None]
-    gain_two, shift_two = ln2_gain.astype(F32)[:, None], ln2_bias.astype(F32)[:, None]
-    d_qkv = (dw[:, :first] * gain_one + shift_one * bias_q).reshape(own, 3, cols)
-    d_fc1 = dw[:, first:edge] * gain_two + shift_two * bias_u
-    d_dense = dw[:, edge : edge + cols].T
-    d_fc2 = dw[:, edge + cols :].T
-    place = (lax.axis_index("fsdp") * nc + lax.axis_index("ctx")) * own
-    d_shift = lax.dynamic_slice_in_dim(sums[0, edge:], place, own)
-    four = norms[:, 0:4].T
     return (
         y_prompt[None],
         y_cont.reshape(shape),
         dx_prompt[None],
         dx_cont.reshape(shape),
-        d_qkv,
-        bias_q.reshape(3, cols),
+        d_qkv.transpose(1, 0, 2),
+        b_qkv,
         d_dense,
         d_shift,
-        d_fc1,
-        bias_u,
-        d_fc2,
+        d_u,
+        b_u.reshape(ff),
+        d_o,
         d_shift,
         four[0],
         four[1],

time: 252 us -> 197 us (0.78)
  Pallas kernels: 218 us -> 193 us
  other arithmetic: 24.4 us -> 0 us
  local copies, waits for them, and re-layouts: 8.47 us -> 2.52 us
    pallas_call x1, Pallas kernels: 218 us -> 182 us  [run_layer(): pl.pallas_call(functools.partial(layer_kernel, sizes), out_shape=shapes,...]
    pallas_call x0 -> x1, Pallas kernels: none -> 11.3 us  [close_layer(): pl.pallas_call(functools.partial(close_kernel, sizes), grid=(blocks,), in...]
    reduce_sum x6 -> x0, other arithmetic: 9.14 us -> none  [the longest x2 4.38 us: finish(): jnp.mean(u, axis=-1, keepdims=True)]
    add x2 -> x0, other arithmetic: 5.63 us -> none  [the longest x1 4.52 us: finish(): return (x + y_rows.astype(F32) + shift, dy.astype(F32) + scale * u)]
    broadcast_in_dim x1 -> x0, other arithmetic: 3.23 us -> none  [on_device(): dx_prompt[None]]
    convert_element_type x4 -> x0, other arithmetic: 2.75 us -> none  [the longest x1 0.78 us: on_device(): ln1_gain.astype(F32)[:, None]]
where the time goes in v3:
time: 197 us
  Pallas kernels  193 us (98%)
  local copies, waits for them, and re-layouts  2.52 us (1%)
    pallas_call x1, Pallas kernels, run_layer(): pl.pallas_call(functools.partial(layer_kernel, sizes), out_shape=shapes,...  182 us
    pallas_call x1, Pallas kernels, close_layer(): pl.pallas_call(functools.partial(close_kernel, sizes), grid=(blocks,), in...  11.3 us

profile of v3, /device:TPU:0, one launch (start us, length us, event | category | flops | bytes accessed | tf_op | source)
XLA Modules:
  0.0 196.5 jit_solution(2267612946134108742)
XLA Ops:
  0.7 182.0 %layer.1 = (bf16[2,1024,1024]{2,1,0:T(8,128)(2,1)}, f32[128,3072]{1,0:T(8,128)}, f32[8,2816]{1,0:T(8,128)}, f32[128,128]{1,0:T(8,128)}, f32[8,1024]{1,0:T(8,128)}) custom-call(s32[1,3]{1,0:T(1,128)} %refs_0_.1, f32[8,128]{1,0:T(8,128)} %constant.2.clone.refs_1_, bf16[256,1024]{1,0:T(8,128)(2,1)} %bitcast.24, bf16[768,1024]{1,0:T(8,128)(2,1)} %bitcast.20, ...), custom_call_target="tpu_custom_call" | custom-call | tf_op jit(solution)/shard_map/layer/pallas_call | solution.py:888
  182.7 11.3 %close.1 = (f32[256,1024]{1,0:T(8,128)}, f32[768,1024]{1,0:T(8,128)}, f32[256,1024]{1,0:T(8,128)}, f32[768,1024]{1,0:T(8,128)}, f32[3,128,256]{2,1,0:T(8,128)}, ...) custom-call(bf16[256,1024]{1,0:T(8,128)(2,1)} %bitcast.25, ...), custom_call_target="tpu_custom_call" | custom-call | tf_op jit(solution)/shard_map/close/pallas_call | solution.py:991
  194.0 1.4 slice_bitcast_fusion
  195.4 1.2 copy.35
